TPU v7x, 512 devices: a whole 4x8x8 slice. The times are simulated.
512 devices in a mesh: gx: 8 (over x, core), gy: 8 (over z), gz: 8 (over y).
Axes of the slice: x: 4, y: 8, z: 8, core: 2. Of those that a mesh axis runs over, the one named last changes fastest.
Arguments:
- rhs: float32 [64, 128, 1024], P('gx', 'gy', 'gz'), may hold values from -5 to 5
- coef: float32 [64, 128, 1024], P('gx', 'gy', 'gz'), may hold values from 0.3 to 3
- agglom: int32 [512, 1], replicated, may hold values from 0 to 63, as said below
Outputs:
- solution: float32 [64, 128, 1024], P('gx', 'gy', 'gz')
Inputs may be any that keep to these rules, and one draw needn't show every extreme that they name: `agglom`: every section device takes at least one block and at most 16; some takes exactly 16. The blocks of one section device are consecutive along the bit-alternated (Morton) order of the block grid, with the third dimension's bit lowest at each level.
All inputs are finite; a program needn't handle non-finite values.
Results may differ from a plain program's by a relative error of at most 0.0003.
Values sent between devices are 32-bit elements; how exact they have to be, the bound alone decides.
A program may use at most 64 MiB of HBM per device.

v0:
```python
import jax
import jax.numpy as jnp
from jax import lax
from jax.sharding import PartitionSpec as P

SLICE_LEVELS = 3
POST = 2
CYCLES = 2
COARSE_SWEEPS = 8
MOST = 16


OMEGA = 0.8
UPPER_LIMIT = lax.Precision.HIGHEST


def padded_2(x, sides, width):
    for axis, dim in sides:
        devices, length = (lax.axis_size(axis), x.shape[dim])
        up = [(i, (i + 1) % devices) for i in range(devices - 1)]
        down = [(j, i) for i, j in up]
        last = lax.slice_in_dim(x, length - width, length, axis=dim)
        leading = lax.slice_in_dim(x, 0, width, axis=dim)
        before = lax.ppermute(last, axis, up)
        after = lax.ppermute(leading, axis, down)
        x = jnp.concatenate([before, x, after], axis=dim)
    return x


def restrict(field):
    a, b, c = field.shape
    return field.reshape(a // 2, 2, b // 2, 2, c // 2, 2).mean(axis=(1, 3, 5))


def prolong(field):
    return jnp.repeat(jnp.repeat(jnp.repeat(field, 2, 0), 2, 1), 2, 2)


def shifted(padded):
    return (
        padded[2:, 1:-1, 1:-1],
        padded[:-2, 1:-1, 1:-1],
        padded[1:-1, 2:, 1:-1],
        padded[1:-1, :-2, 1:-1],
        padded[1:-1, 1:-1, 2:],
        padded[1:-1, 1:-1, :-2],
    )


def face_weights(coeffs, padded):
    return tuple((0.5 * (coeffs + other) for other in shifted(padded)))


def weighted(weights, others):
    total = weights[0] * others[0]
    for j in range(1, 6):
        total = total + weights[j] * others[j]
    return total


def diagonal_of(weights, factor):
    total = weights[0]
    for j in range(1, 6):
        total = total + weights[j]
    return factor * total


def lookup(table, wanted):
    positions = jnp.arange(table.shape[0], dtype=jnp.int32)
    return jnp.sum(jnp.where(wanted[:, None] == positions[None, :], table[None, :], 0), axis=1)


def linked_values(errors, links, axis, forward):
    count = errors.shape[0]
    others = jnp.dot(links, errors.reshape(count, -1), precision=UPPER_LIMIT).reshape(errors.shape)
    length = errors.shape[axis + 1]
    if forward:
        return jnp.concatenate(
            (
                lax.slice_in_dim(errors, 1, length, axis=axis + 1),
                lax.slice_in_dim(others, 0, 1, axis=axis + 1),
            ),
            axis=axis + 1,
        )
    return jnp.concatenate(
        (
            lax.slice_in_dim(others, length - 1, length, axis=axis + 1),
            lax.slice_in_dim(errors, 0, length - 1, axis=axis + 1),
        ),
        axis=axis + 1,
    )


def shards(rhs, coef, agglom):
    levels = SLICE_LEVELS
    coeffs = [coef]
    for j in range(levels):
        coeffs.append(restrict(coeffs[-1]))
    weights = []
    diagonals = []
    for j in range(levels + 1):
        padded = padded_2(coeffs[j], (("gx", 0), ("gy", 1), ("gz", 2)), 1)
        level_weights = face_weights(coeffs[j], padded)
        weights.append(level_weights)
        diagonals.append(diagonal_of(level_weights, 0.25**j))
    owners = agglom[:, 0]
    numbers = jnp.arange(owners.shape[0], dtype=jnp.int32)
    same_owner = owners[:, None] == owners[None, :]
    ranks = jnp.sum(same_owner & (numbers[None, :] < numbers[:, None]), axis=1)
    size_x = lax.axis_size("gx")
    size_y = lax.axis_size("gy")
    size_z = lax.axis_size("gz")
    section_me = lax.axis_index("gx") * size_y + lax.axis_index("gy")
    block_me = section_me * size_z + lax.axis_index("gz")
    slot_ids = jnp.arange(MOST, dtype=jnp.int32)
    table = (owners[None, :] == section_me) & (ranks[None, :] == slot_ids[:, None])
    lookup_table_real = table.astype(jnp.float32)
    occupied = jnp.any(table, axis=1)
    slot_block = jnp.sum(jnp.where(table, numbers[None, :], 0), axis=1)
    strides = (size_y * size_z, size_z, 1)
    counts = (size_x, size_y, size_z)
    links = []
    for axis in range(3):
        coord = slot_block // strides[axis] % counts[axis]
        for forward in (True, False):
            if forward:
                inside_grid = coord + 1 < counts[axis]
                target = slot_block + strides[axis]
            else:
                inside_grid = coord > 0
                target = slot_block - strides[axis]
            live = occupied & inside_grid & (lookup(owners, target) == section_me)
            links.append(
                (live[:, None] & (lookup(ranks, target)[:, None] == slot_ids[None, :])).astype(
                    jnp.float32
                )
            )
    my_owner = lookup(owners, block_me[None])[0]
    my_slot = lookup(ranks, block_me[None])[0]
    coarse_shape = coeffs[levels].shape
    cells = coarse_shape[0] * coarse_shape[1] * coarse_shape[2]
    coarse_factor = 0.25**levels
    coarse_weights = jnp.stack(weights[levels]).reshape(1, 6, cells)
    block_shape = (MOST,) + coarse_shape

    def collect(fragment_part):
        return jnp.einsum("vm,mlg->vlg", lookup_table_real, fragment_part, precision=UPPER_LIMIT)

    def pick(fragment_part):
        rows = lax.dynamic_index_in_dim(fragment_part, my_slot, 1, keepdims=False)
        hits = (jnp.arange(fragment_part.shape[0], dtype=jnp.int32) == my_owner).astype(jnp.float32)
        return jnp.dot(hits, rows, precision=UPPER_LIMIT)

    def coarse_correct(source):
        flat = source.reshape(1, 1, cells)
        collected_values = collect(
            lax.all_gather(
                jnp.concatenate((flat, coarse_weights), axis=1),
                ("gx", "gy", "gz"),
                axis=0,
                tiled=True,
            )
        )
        slot_source = collected_values[:, 0]
        slot_face = collected_values[:, 1:]
        slot_source = slot_source.reshape(block_shape)
        face_list = tuple((slot_face[:, j].reshape(block_shape) for j in range(6)))
        diagonal = diagonal_of(face_list, coarse_factor)
        diagonal = jnp.where(occupied[:, None, None, None], diagonal, 1.0)
        errors = OMEGA * slot_source / diagonal
        for j in range(COARSE_SWEEPS - 1):
            others = (
                linked_values(errors, links[0], 0, True),
                linked_values(errors, links[1], 0, False),
                linked_values(errors, links[2], 1, True),
                linked_values(errors, links[3], 1, False),
                linked_values(errors, links[4], 2, True),
                linked_values(errors, links[5], 2, False),
            )
            coupled = weighted(face_list, others)
            errors = (
                errors
                + OMEGA * (slot_source - (diagonal * errors - coarse_factor * coupled)) / diagonal
            )
        errors_flat = errors.reshape(MOST, cells)
        mine = pick(lax.all_gather(errors_flat[None], ("gx", "gy"), axis=0, tiled=True))
        return mine.reshape(coarse_shape)

    def operate(values, level):
        padded = padded_2(values, (("gx", 0), ("gy", 1), ("gz", 2)), 1)
        return diagonals[level] * values - 0.25**level * weighted(weights[level], shifted(padded))

    def smooth(values, source, level):
        return values + OMEGA * (source - operate(values, level)) / diagonals[level]

    def vcycle(source, level):
        if level == levels:
            return coarse_correct(source)
        values = OMEGA * source / diagonals[level]
        values = smooth(values, source, level)
        residual = source - operate(values, level)
        values = values + prolong(vcycle(restrict(residual), level + 1))
        for j in range(POST):
            values = smooth(values, source, level)
        return values

    solution = jnp.zeros_like(rhs)
    for cycle in range(CYCLES):
        residual = rhs if cycle == 0 else rhs - operate(solution, 0)
        solution = solution + vcycle(residual, 0)
    return solution


def solution(mesh):
    in_specs = (P("gx", "gy", "gz"), P("gx", "gy", "gz"), P())
    out_specs = P("gx", "gy", "gz")
    return jax.shard_map(shards, mesh=mesh, in_specs=in_specs, out_specs=out_specs, check_vma=False)
```

profile of v0, /device:TPU:1, one launch (start us, length us, event | category | flops | bytes accessed | tf_op | source)
XLA Modules:
  0.0 1005.6 jit_solution(9172164788637455164)
XLA Ops:
  0.0 6.3 reshape.1506
  9.7 4.5 collective-permute-start.55
  14.2 5.5 collective-permute-start.54
  53.2 4.8 collective-permute-start.7
  65.3 5.8 collective-permute-start.9
  72.5 4.5 collective-permute-done.8
  85.1 5.6 collective-permute-start.13
  107.5 5.6 collective-permute-start.17
  115.5 5.5 reshape.1505
  123.6 4.2 collective-permute-start.25
  129.7 4.5 collective-permute-start.57
  135.6 5.5 collective-permute-start.27
  147.5 5.5 collective-permute-start.29
  157.8 5.9 collective-permute-start.31
  168.7 4.4 collective-permute-start.33
  174.5 4.5 collective-permute-done.32
  180.3 5.9 collective-permute-start.35
  186.3 5.1 collective-permute-start.41
  193.5 4.8 collective-permute-done.40
  217.0 5.5 collective-permute-start.47
  244.9 4.9 collective-permute-start.53
  251.0 77.8 %all_gather.12 = f32[512,7,32]{2,1,0:T(8,128)S(1)} all-gather(f32[1,7,32]{2,1,0:T(8,128)S(1)} %concatenate.1254), channel_id=1, replica_groups=mesh['gx'=8,'gy'=8,'gz'=8] {'gx','gy','gz'}, dimensions={0}, use_global_device_ids=true | all-gather | bytes 459648 | tf_op jit(solution)/shard_map/all_gather | solution.py:157
  339.9 49.5 %all_gather.13 = f32[64,16,32]{2,1,0:T(8,128)S(1)} all-gather(f32[1,16,32]{2,1,0:T(8,128)S(1)} %copy.1492), channel_id=1, replica_groups=mesh['gx'=8,'gy'=8,'gz'=8] {'gx','gy'}, dimensions={0}, use_global_device_ids=true | all-gather | bytes 133120 | tf_op jit(solution)/shard_map/all_gather | solution.py:186
  412.1 4.2 collective-permute-start.67
  430.6 4.5 collective-permute-start.71
  436.4 4.2 collective-permute-start.73
  455.6 4.5 collective-permute-start.77
  479.7 4.6 collective-permute-start.83
  503.9 4.6 collective-permute-start.89
  528.3 5.4 collective-permute-start.95
  553.7 5.8 collective-permute-start.101
  579.3 5.8 collective-permute-start.107
  605.0 6.1 collective-permute-start.113
  614.2 5.5 reshape.1521
  638.8 5.9 collective-permute-start.119
  663.7 5.9 collective-permute-start.125
  689.2 5.9 collective-permute-start.131
  696.1 4.2 collective-permute-start.133
  713.8 5.9 collective-permute-start.137
  721.0 77.7 %all_gather.14 = f32[512,7,32]{2,1,0:T(8,128)S(1)} all-gather(f32[1,7,32]{2,1,0:T(8,128)S(1)} %concatenate.1443), channel_id=1, replica_groups=mesh['gx'=8,'gy'=8,'gz'=8] {'gx','gy','gz'}, dimensions={0}, use_global_device_ids=true | all-gather | bytes 459648 | tf_op jit(solution)/shard_map/all_gather | solution.py:157
  809.8 49.1 %all_gather.15 = f32[64,16,32]{2,1,0:T(8,128)S(1)} all-gather(f32[1,16,32]{2,1,0:T(8,128)S(1)} %copy.1604), channel_id=1, replica_groups=mesh['gx'=8,'gy'=8,'gz'=8] {'gx','gy'}, dimensions={0}, use_global_device_ids=true | all-gather | bytes 133120 | tf_op jit(solution)/shard_map/all_gather | solution.py:186
  880.9 4.5 collective-permute-start.145
  899.3 4.5 collective-permute-start.149
  905.1 4.2 collective-permute-start.151
  924.3 4.5 collective-permute-start.155
  948.4 4.6 collective-permute-start.161
  972.5 4.6 collective-permute-start.167
  997.0 4.7 collective-permute-start.173
  (780 shorter events, 521.8 us)
Async XLA Ops:
  9.7 26.3 %collective-permute-start.55 = (f32[1,2,16]{2,1,0:T(2,128)S(1)}, f32[1,2,16]{2,1,0:T(2,128)S(1)}, u32[]{:S(2)}, u32[]{:S(2)}) collective-permute-start(f32[1,2,16]{2,1,0:T(2,128)S(1)} %multiply_bitcast_fusion), channel_id=1, source_target_pairs={{0,64},{64,128},{128,192},{192,256},{256,320},{320,384},{384,448},... | collective-permute-start | bytes 392 | tf_op jit(solution)/shard_map/ppermute | solution.py:24
  14.2 23.4 %collective-permute-start.54 = (f32[1,2,16]{2,1,0:T(2,128)S(1)}, f32[1,2,16]{2,1,0:T(2,128)S(1)}, u32[]{:S(2)}, u32[]{:S(2)}) collective-permute-start(f32[1,2,16]{2,1,0:T(2,128)S(1)} %multiply_bitcast_fusion), channel_id=1, source_target_pairs={{64,0},{128,64},{192,128},{256,192},{320,256},{384,320},{448,384},... | collective-permute-start | bytes 392 | tf_op jit(solution)/shard_map/ppermute | solution.py:25
  19.8 10.5 %collective-permute-start.1 = (f32[1,16,128]{2,1,0:T(8,128)S(1)}, f32[1,16,128]{2,1,0:T(8,128)S(1)}, u32[]{:S(2)}, u32[]{:S(2)}) collective-permute-start(f32[1,16,128]{2,1,0:T(8,128)S(1)} %get-tuple-element.110), channel_id=1, source_target_pairs={{0,64},{64,128},{128,192},{192,256},{256,320},{320,384},{384,448},... | collective-permute-start | bytes 24584 | tf_op jit(solution)/shard_map/ppermute | solution.py:24
  21.7 12.3 %collective-permute-start = (f32[1,16,128]{2,1,0:T(8,128)S(1)}, f32[1,16,128]{2,1,0:T(8,128)S(1)}, u32[]{:S(2)}, u32[]{:S(2)}) collective-permute-start(f32[1,16,128]{2,1,0:T(8,128)S(1)} %get-tuple-element.111), channel_id=1, source_target_pairs={{64,0},{128,64},{192,128},{256,192},{320,256},{384,320},{448,384},... | collective-permute-start | bytes 24584 | tf_op jit(solution)/shard_map/ppermute | solution.py:25
  24.2 22.1 %collective-permute-start.18 = (f32[1,8,64]{2,1,0:T(8,128)S(1)}, f32[1,8,64]{2,1,0:T(8,128)S(1)}, u32[]{:S(2)}, u32[]{:S(2)}) collective-permute-start(f32[1,8,64]{2,1,0:T(8,128)S(1)} %get-tuple-element.272), channel_id=1, source_target_pairs={{64,0},{128,64},{192,128},{256,192},{320,256},{384,320},{448,384},... | collective-permute-start | bytes 6152 | tf_op jit(solution)/shard_map/ppermute | solution.py:25
  30.4 17.2 %collective-permute-start.19 = (f32[1,8,64]{2,1,0:T(8,128)S(1)}, f32[1,8,64]{2,1,0:T(8,128)S(1)}, u32[]{:S(2)}, u32[]{:S(2)}) collective-permute-start(f32[1,8,64]{2,1,0:T(8,128)S(1)} %get-tuple-element.273), channel_id=1, source_target_pairs={{0,64},{64,128},{128,192},{192,256},{256,320},{320,384},{384,448},... | collective-permute-start | bytes 6152 | tf_op jit(solution)/shard_map/ppermute | solution.py:24
  34.0 107.1 %collective-permute-start.36 = (f32[1,4,32]{2,1,0:T(4,128)S(1)}, f32[1,4,32]{2,1,0:T(4,128)S(1)}, u32[]{:S(2)}, u32[]{:S(2)}) collective-permute-start(f32[1,4,32]{2,1,0:T(4,128)S(1)} %get-tuple-element.315), channel_id=1, source_target_pairs={{64,0},{128,64},{192,128},{256,192},{320,256},{384,320},{448,384},... | collective-permute-start | bytes 1544 | tf_op jit(solution)/shard_map/ppermute | solution.py:25
  39.0 102.2 %collective-permute-start.37 = (f32[1,4,32]{2,1,0:T(4,128)S(1)}, f32[1,4,32]{2,1,0:T(4,128)S(1)}, u32[]{:S(2)}, u32[]{:S(2)}) collective-permute-start(f32[1,4,32]{2,1,0:T(4,128)S(1)} %get-tuple-element.316), channel_id=1, source_target_pairs={{0,64},{64,128},{128,192},{192,256},{256,320},{320,384},{384,448},... | collective-permute-start | bytes 1544 | tf_op jit(solution)/shard_map/ppermute | solution.py:24
  53.2 10.8 %collective-permute-start.7 = (f32[1,16,128]{2,1,0:T(8,128)S(1)}, f32[1,16,128]{2,1,0:T(8,128)S(1)}, u32[]{:S(2)}, u32[]{:S(2)}) collective-permute-start(f32[1,16,128]{2,1,0:T(8,128)S(1)} %get-tuple-element.108), channel_id=1, source_target_pairs={{0,64},{64,128},{128,192},{192,256},{256,320},{320,384},{384,448},... | collective-permute-start | bytes 24584 | tf_op jit(solution)/shard_map/ppermute | solution.py:24
  58.0 7.3 collective-permute-start.6
  60.0 11.2 %collective-permute-start.21 = (f32[6,1,64]{2,1,0:T(1,128)S(1)}, f32[6,1,64]{2,1,0:T(1,128)S(1)}, u32[]{:S(2)}, u32[]{:S(2)}) collective-permute-start(f32[6,1,64]{2,1,0:T(1,128)S(1)} %get-tuple-element.180), channel_id=1, source_target_pairs={{0,8},{8,16},{16,24},{24,32},{32,40},{40,48},{48,56},{1,9},{9,17},... | collective-permute-start | bytes 4616 | tf_op jit(solution)/shard_map/ppermute | solution.py:24
  64.0 28.6 %collective-permute-start.20 = (f32[6,1,64]{2,1,0:T(1,128)S(1)}, f32[6,1,64]{2,1,0:T(1,128)S(1)}, u32[]{:S(2)}, u32[]{:S(2)}) collective-permute-start(f32[6,1,64]{2,1,0:T(1,128)S(1)} %get-tuple-element.181), channel_id=1, source_target_pairs={{8,0},{16,8},{24,16},{32,24},{40,32},{48,40},{56,48},{9,1},{17,9},... | collective-permute-start | bytes 4616 | tf_op jit(solution)/shard_map/ppermute | solution.py:25
  85.1 7.5 collective-permute-start.13
  95.7 9.1 collective-permute-start.15
  104.8 8.3 collective-permute-start.22
  106.2 7.4 collective-permute-start.16
  107.5 7.8 collective-permute-start.17
  123.6 10.7 %collective-permute-start.25 = (f32[1,8,64]{2,1,0:T(8,128)S(1)}, f32[1,8,64]{2,1,0:T(8,128)S(1)}, u32[]{:S(2)}, u32[]{:S(2)}) collective-permute-start(f32[1,8,64]{2,1,0:T(8,128)S(1)} %get-tuple-element.270), channel_id=1, source_target_pairs={{0,64},{64,128},{128,192},{192,256},{256,320},{320,384},{384,448},... | collective-permute-start | bytes 6152 | tf_op jit(solution)/shard_map/ppermute | solution.py:24
  127.8 7.8 collective-permute-start.24
  129.7 74.7 %collective-permute-start.57 = (f32[3,1,16]{2,1,0:T(1,128)S(1)}, f32[3,1,16]{2,1,0:T(1,128)S(1)}, u32[]{:S(2)}, u32[]{:S(2)}) collective-permute-start(f32[3,1,16]{2,1,0:T(1,128)S(1)} %get-tuple-element.317), channel_id=1, source_target_pairs={{0,8},{8,16},{16,24},{24,32},{32,40},{40,48},{48,56},{1,9},{9,17},... | collective-permute-start | bytes 584 | tf_op jit(solution)/shard_map/ppermute | solution.py:24
  134.3 70.1 %collective-permute-start.56 = (f32[3,1,16]{2,1,0:T(1,128)S(1)}, f32[3,1,16]{2,1,0:T(1,128)S(1)}, u32[]{:S(2)}, u32[]{:S(2)}) collective-permute-start(f32[3,1,16]{2,1,0:T(1,128)S(1)} %get-tuple-element.318), channel_id=1, source_target_pairs={{8,0},{16,8},{24,16},{32,24},{40,32},{48,40},{56,48},{9,1},{17,9},... | collective-permute-start | bytes 584 | tf_op jit(solution)/shard_map/ppermute | solution.py:25
  146.2 10.1 %collective-permute-start.28 = (f32[6,10,1]{2,0,1:T(8,128)S(1)}, f32[6,10,1]{2,0,1:T(8,128)S(1)}, u32[]{:S(2)}, u32[]{:S(2)}) collective-permute-start(f32[6,10,1]{2,0,1:T(8,128)S(1)} %get-tuple-element.158), channel_id=1, source_target_pairs={{1,0},{2,1},{3,2},{4,3},{5,4},{6,5},{7,6},{9,8},{10,9},{11,10},{12... | collective-permute-start | bytes 728 | tf_op jit(solution)/shard_map/ppermute | solution.py:25
  147.5 10.2 %collective-permute-start.29 = (f32[6,10,1]{2,0,1:T(8,128)S(1)}, f32[6,10,1]{2,0,1:T(8,128)S(1)}, u32[]{:S(2)}, u32[]{:S(2)}) collective-permute-start(f32[6,10,1]{2,0,1:T(8,128)S(1)} %get-tuple-element.159), channel_id=1, source_target_pairs={{0,1},{1,2},{2,3},{3,4},{4,5},{5,6},{6,7},{8,9},{9,10},{10,11},{11... | collective-permute-start | bytes 728 | tf_op jit(solution)/shard_map/ppermute | solution.py:24
  152.9 10.8 %collective-permute-start.39 = (f32[4,1,32]{2,1,0:T(1,128)S(1)}, f32[4,1,32]{2,1,0:T(1,128)S(1)}, u32[]{:S(2)}, u32[]{:S(2)}) collective-permute-start(f32[4,1,32]{2,1,0:T(1,128)S(1)} %get-tuple-element.290), channel_id=1, source_target_pairs={{0,8},{8,16},{16,24},{24,32},{32,40},{40,48},{48,56},{1,9},{9,17},... | collective-permute-start | bytes 1544 | tf_op jit(solution)/shard_map/ppermute | solution.py:24
  156.3 9.3 collective-permute-start.38
  157.8 7.9 collective-permute-start.31
  179.0 12.3 %collective-permute-start.34 = (f32[6,10,1]{2,0,1:T(8,128)S(1)}, f32[6,10,1]{2,0,1:T(8,128)S(1)}, u32[]{:S(2)}, u32[]{:S(2)}) collective-permute-start(f32[6,10,1]{2,0,1:T(8,128)S(1)} %get-tuple-element.154), channel_id=1, source_target_pairs={{1,0},{2,1},{3,2},{4,3},{5,4},{6,5},{7,6},{9,8},{10,9},{11,10},{12... | collective-permute-start | bytes 728 | tf_op jit(solution)/shard_map/ppermute | solution.py:25
  180.3 12.4 %collective-permute-start.35 = (f32[6,10,1]{2,0,1:T(8,128)S(1)}, f32[6,10,1]{2,0,1:T(8,128)S(1)}, u32[]{:S(2)}, u32[]{:S(2)}) collective-permute-start(f32[6,10,1]{2,0,1:T(8,128)S(1)} %get-tuple-element.155), channel_id=1, source_target_pairs={{0,1},{1,2},{2,3},{3,4},{4,5},{5,6},{6,7},{8,9},{9,10},{10,11},{11... | collective-permute-start | bytes 728 | tf_op jit(solution)/shard_map/ppermute | solution.py:24
  186.3 7.3 collective-permute-start.41
  223.5 11.3 %collective-permute-start.49 = (f32[1,4,32]{2,1,0:T(4,128)S(1)}, f32[1,4,32]{2,1,0:T(4,128)S(1)}, u32[]{:S(2)}, u32[]{:S(2)}) collective-permute-start(f32[1,4,32]{2,1,0:T(4,128)S(1)} %get-tuple-element.311), channel_id=1, source_target_pairs={{0,64},{64,128},{128,192},{192,256},{256,320},{320,384},{384,448},... | collective-permute-start | bytes 1544 | tf_op jit(solution)/shard_map/ppermute | solution.py:24
  227.4 7.3 collective-permute-start.48
  229.5 10.6 %collective-permute-start.59 = (f32[3,4,1]{2,1,0:T(4,128)S(1)}, f32[3,4,1]{2,1,0:T(4,128)S(1)}, u32[]{:S(2)}, u32[]{:S(2)}) collective-permute-start(f32[3,4,1]{2,1,0:T(4,128)S(1)} %get-tuple-element.294), channel_id=1, source_target_pairs={{0,1},{1,2},{2,3},{3,4},{4,5},{5,6},{6,7},{8,9},{9,10},{10,11},{11... | collective-permute-start | bytes 152 | tf_op jit(solution)/shard_map/ppermute | solution.py:24
  502.6 7.3 collective-permute-start.88
  503.9 7.7 collective-permute-start.89
  527.0 8.1 collective-permute-start.94
  528.3 8.6 collective-permute-start.95
  552.4 8.5 collective-permute-start.100
  553.7 8.9 collective-permute-start.101
  578.0 8.5 collective-permute-start.106
  579.3 8.9 collective-permute-start.107
  603.7 8.6 collective-permute-start.112
  605.0 9.0 collective-permute-start.113
  638.8 7.2 collective-permute-start.119
  663.7 7.2 collective-permute-start.125
  971.2 7.3 collective-permute-start.166
  972.5 7.7 collective-permute-start.167
  995.7 7.4 collective-permute-start.172
  997.0 7.8 collective-permute-start.173
  (129 other events, 739.9 us)
where the time goes:
time: 1020 us; the launch traced here: 1010 us
  starting transfers between devices  490 us (48%)
  blocking collectives  254 us (25%)
  waiting for transfers between devices  193 us (19%)
  local copies, waits for them, and re-layouts  26.5 us (3%)
  matrix products  20.7 us (2%)
  other arithmetic  15.7 us (2%)
    ppermute x87, starting transfers between devices, padded_2(): before = lax.ppermute(last, axis, up)  354 us
    ppermute x87, waiting for transfers between devices, padded_2(): after = lax.ppermute(leading, axis, down)  161 us
    all_gather x2, blocking collectives, coarse_correct(): lax.all_gather(jnp.concatenate((flat, coarse_weights), axis=1), ('gx', 'g...  155 us
    ppermute x87, starting transfers between devices, padded_2(): after = lax.ppermute(leading, axis, down)  136 us
    all_gather x2, blocking collectives, coarse_correct(): lax.all_gather(errors_flat[None], ('gx', 'gy'), axis=0, tiled=True)  98.5 us
    ppermute x87, waiting for transfers between devices, padded_2(): before = lax.ppermute(last, axis, up)  31.4 us
  transfers between devices with their start and end apart: 174, of which 81 were waited for; matrix products, arithmetic and copies ran while one was open for 1% of the time, Pallas kernels for 0%

commit v1 on v0

v1 whole, which is shorter than its diff:
```python
import jax
import jax.numpy as jnp
import numpy as np
from jax import lax
from jax.experimental import pallas as pl
from jax.experimental.pallas import tpu as pltpu
from jax.sharding import PartitionSpec as P

F32 = jnp.float32
BF16 = jnp.bfloat16
MESH = pl.DeviceIdType.MESH
OUT = -100000
COARSE_SWEEPS = 8
DIRS = [(dx, dy) for dx in (-1, 0, 1) for dy in (-1, 0, 1) if (dx, dy) != (0, 0)]
FAR = [(dx, dy) for dx in (-2, 2) for dy in (-1, 0, 1)]
XE0, YE0, H0 = 16, 24, 4
XE1, YE1, H1 = 14, 18, 5
L0, L1 = 384, 256
R0, R1, R2, R3 = 144, 80, 96, 48


def up128(n):
    return -(-n // 128) * 128


def lane0(x, y):
    return (y + H0) * XE0 + x + H0


def lane1(x, y):
    return (y + H1) * XE1 + x + H1


def tables(nx, ny):
    x2, y2 = 2 * nx, 4 * ny
    l2, l3 = up128(x2 * y2), up128(nx * 2 * ny)
    t = {}
    place0 = np.zeros((512, L0), np.float32)
    sel0 = np.zeros((32, L0), np.float32)
    unsel = np.zeros((128, L0), np.float32)
    for x in range(8):
        for y in range(16):
            place0[x * 16 + y, lane0(x, y)] = 1
            unsel[x * 16 + y, lane0(x, y)] = 1
            sel0[(x // 2) * 8 + y // 2, lane0(x, y)] = 0.125
    for s in range(2):
        for xi in range(4):
            for y in range(16):
                place0[128 + s * 64 + xi * 16 + y, lane0(xi - 4 if s == 0 else 8 + xi, y)] = 1
        for x in range(8):
            for yi in range(8):
                yy = yi - 8 if s == 0 else 16 + yi
                if -H0 <= yy < 16 + H0:
                    place0[256 + s * 64 + x * 8 + yi, lane0(x, yy)] = 1
        for q in range(2):
            for xi in range(4):
                for yi in range(8):
                    yy = yi - 8 if q == 0 else 16 + yi
                    if -H0 <= yy < 16 + H0:
                        place0[384 + (s * 2 + q) * 32 + xi * 8 + yi, lane0(xi - 4 if s == 0 else 8 + xi, yy)] = 1
    place1 = np.zeros((384, L1), np.float32)
    for d, (sx, sy) in enumerate([(0, 0)] + DIRS):
        for x in range(4):
            for y in range(8):
                xx, yy = x + 4 * sx, y + 8 * sy
                if -H1 <= xx < 4 + H1 and -H1 <= yy < 8 + H1:
                    place1[32 * d + x * 8 + y, lane1(xx, yy)] = 1
    for e, (sx, sy) in enumerate(FAR):
        for y in range(8):
            xx, yy = (-5 if sx < 0 else 8), y + 8 * sy
            if -H1 <= yy < 8 + H1:
                place1[288 + 8 * e + y, lane1(xx, yy)] = 1
    sel1 = np.zeros((8, L1), np.float32)
    for x in range(4):
        for y in range(8):
            sel1[(x // 2) * 4 + y // 2, lane1(x, y)] = 0.125
    prol0 = np.zeros((L1, L0), np.float32)
    for x in range(-H0, 8 + H0):
        for y in range(-H0, 16 + H0):
            prol0[lane1(x // 2, y // 2), lane0(x, y)] = 1
    perm2 = np.zeros((nx * ny * 8, l2), np.float32)
    for a in range(nx):
        for b in range(ny):
            for i in range(2):
                for j in range(4):
                    perm2[(a * ny + b) * 8 + i * 4 + j, (b * 4 + j) * x2 + a * 2 + i] = 1
    rest2 = np.zeros((l2, l3), np.float32)
    own3 = np.zeros((128, l3), np.float32)
    for x in range(x2):
        for y in range(y2):
            rest2[y * x2 + x, (y // 2) * nx + x // 2] = 0.125
    for x in range(nx):
        for y in range(2 * ny):
            own3[x * ny + y // 2, y * nx + x] = 1
    prol2 = (rest2.T != 0).astype(np.float32)
    kx1 = np.zeros((32, 128), np.float32)
    kx2 = np.zeros((8, 128), np.float32)
    for x in range(8):
        for y in range(16):
            kx1[(x // 2) * 8 + y // 2, x * 16 + y] = 0.25
            kx2[(x // 4) * 4 + y // 4, x * 16 + y] = 0.0625
    kz1 = np.zeros((128, 128), np.float32)
    kz2 = np.zeros((128, 128), np.float32)
    for z in range(128):
        kz1[z, z // 2] = 0.5
        for c in range(3):
            kz2[z, 32 * c + z // 4] = 0.25
    coord = np.full((16, max(L0, l2)), OUT, np.int32)
    for x in range(-H0, 8 + H0):
        for y in range(-H0, 16 + H0):
            coord[0:2, lane0(x, y)] = x, y
    for x in range(-H1, 4 + H1):
        for y in range(-H1, 8 + H1):
            coord[2:4, lane1(x, y)] = x, y
            coord[8, lane1(x, y)] = (y // 2) * x2 + x // 2
    for x in range(x2):
        for y in range(y2):
            coord[4:6, y * x2 + x] = x, y
    for x in range(nx):
        for y in range(2 * ny):
            coord[6:8, y * nx + x] = x, y
    names = dict(place0=place0, sel0=sel0, unsel=unsel, place1=place1, sel1=sel1, prol0=prol0, perm2=perm2, rest2=rest2,
                 own3=own3, prol2=prol2, kx1=kx1, kx2=kx2, kz1=kz1, kz2=kz2)
    t = {k: v.astype(jnp.bfloat16) for k, v in names.items()}
    t["coord"] = coord
    return t


def split(x):
    hi = x.astype(BF16)
    return hi, (x - hi.astype(F32)).astype(BF16)


def times(x, w):
    rows = x.shape[0]
    both = jnp.dot(jnp.concatenate(split(x), axis=0), w, preferred_element_type=F32)
    return both[:rows] + both[rows:]


def select_t(w, x):
    dims = (((1,), (1,)), ((), ()))
    hi, lo = split(x)
    return lax.dot_general(w, hi, dims, preferred_element_type=F32) + lax.dot_general(w, lo, dims, preferred_element_type=F32)


def left(w, x):
    hi, lo = split(x)
    return jnp.dot(w, hi, preferred_element_type=F32) + jnp.dot(w, lo, preferred_element_type=F32)


def build(nx, ny, nz):
    x2, y2 = 2 * nx, 4 * ny
    l2, l3 = up128(x2 * y2), up128(nx * 2 * ny)
    consts = tables(nx, ny)
    names = list(consts)

    n_sem = 3 * 10 + 3 * 16 + 3 * (2 + nx + ny)

    scratch = dict(
        xs0=pltpu.VMEM((3, 2, 4, 16, 128), F32),
        ys0=pltpu.VMEM((3, 2, 8, 8, 128), F32),
        ds0=pltpu.VMEM((3, 4, 4, 8, 128), F32),
        ext0=pltpu.VMEM((3, R0, L0), F32),
        nat1=pltpu.VMEM((3, 48, 8, 128), F32),
        ext1=pltpu.VMEM((3, R1, L1), F32),
        own2=pltpu.VMEM((3, 8, 128), F32),
        zs2=pltpu.VMEM((3, 2, 8, 128), F32),
        ys2=pltpu.VMEM((3, ny, 8, 128), F32),
        xs2=pltpu.VMEM((3, nx, ny, 8, 128), F32),
        sol=pltpu.VMEM((8, 16, 128), F32),
        m0=pltpu.VMEM((6, R0, L0), F32),
        c0=pltpu.VMEM((4, R0, L0), F32),
        m1=pltpu.VMEM((6, R1, L1), F32),
        c1=pltpu.VMEM((4, R1, L1), F32),
        m2=pltpu.VMEM((6, R2, l2), F32),
        c2=pltpu.VMEM((4, R2, l2), F32),
        m3=pltpu.VMEM((6, R3, l3), F32),
        c3=pltpu.VMEM((2, R3, l3), F32),
        pairs=pltpu.VMEM((max(L0, l2) // 128, 160, 128), F32),
        prol1=pltpu.VMEM((l2, L1), BF16),
        owners=pltpu.VMEM((8, l3), F32),
        ssem=pltpu.SemaphoreType.DMA((n_sem,)),
        rsem=pltpu.SemaphoreType.DMA((n_sem,)),
    )
    keys = list(scratch)

    def kernel(rhs, coef, agg, *rest):
        c = dict(zip(names, rest[: len(names)]))
        out = rest[len(names)]
        s = dict(zip(keys, rest[len(names) + 1:]))
        gx, gy, gz = lax.axis_index("gx"), lax.axis_index("gy"), lax.axis_index("gz")

        def has(dx, dy, dz):
            ok = None
            for g, d, n in ((gx, dx, nx), (gy, dy, ny), (gz, dz, nz)):
                if d:
                    here = (g + d >= 0) if d < 0 else (g + d < n)
                    ok = here if ok is None else ok & here
            return ok

        counter = [0]
        unsent = []

        class Copy:
            def __init__(self, src, dst, there, send_if, recv_if):
                i = counter[0]
                counter[0] += 1
                self.make = lambda: pltpu.make_async_remote_copy(
                    src_ref=src, dst_ref=dst, send_sem=s["ssem"].at[i], recv_sem=s["rsem"].at[i],
                    device_id=there, device_id_type=MESH)
                self.send_if, self.recv_if = send_if, recv_if
                unsent.append(self)

            def under(self, cond, f):
                if cond is None:
                    f()
                else:
                    pl.when(cond)(f)

            def start(self):
                self.under(self.send_if, lambda: self.make().start())

            def arrive(self):
                self.under(self.recv_if, lambda: self.make().wait_recv())

            def sent(self):
                self.under(self.send_if, lambda: self.make().wait_send())

        def toward(dx, dy, dz, src, dst):
            return Copy(src, dst, (gx + dx, gy + dy, gz + dz), has(dx, dy, dz), has(-dx, -dy, -dz))

        def plane0(n, src):
            copies = []
            for dx, dy in DIRS:
                xs = slice(0, 8) if dx == 0 else (slice(4, 8) if dx > 0 else slice(0, 4))
                ys = slice(0, 16) if dy == 0 else (slice(8, 16) if dy > 0 else slice(0, 8))
                a, b = (0 if dx > 0 else 1), (0 if dy > 0 else 1)
                if dy == 0:
                    dst = s["xs0"].at[n, a]
                elif dx == 0:
                    dst = s["ys0"].at[n, b]
                else:
                    dst = s["ds0"].at[n, 2 * a + b]
                copies.append(toward(dx, dy, 0, src.at[xs, ys, :], dst))
            return copies

        def z_halo(ref, n, rows):
            return [toward(0, 0, -1, ref.at[n, 8:16, :], ref.at[n, rows - 8:rows, :]),
                    toward(0, 0, 1, ref.at[n, rows - 16:rows - 8, :], ref.at[n, 0:8, :])]

        def plane1(n, far):
            copies = []
            for dx, dy in DIRS:
                d = 1 + DIRS.index((-dx, -dy))
                copies.append(toward(dx, dy, 0, s["nat1"].at[n, 0:4], s["nat1"].at[n, 4 * d:4 * d + 4]))
            if far:
                for dx, dy in FAR:
                    e = FAR.index((-dx, -dy))
                    i = 3 if dx > 0 else 0
                    copies.append(toward(dx, dy, 0, s["nat1"].at[n, i:i + 1], s["nat1"].at[n, 36 + e:37 + e]))
            return copies

        def z2(n):
            return [toward(0, 0, -1, s["own2"].at[n], s["zs2"].at[n, 1]),
                    toward(0, 0, 1, s["own2"].at[n], s["zs2"].at[n, 0])]

        def y2line(n):
            return [Copy(s["ys2"].at[n, gy], s["ys2"].at[n, gy], (gx, lax.rem(gy + d, ny), gz), None, None)
                    for d in range(1, ny)]

        def x2line(n):
            return [Copy(s["ys2"].at[n], s["xs2"].at[n, gx], (lax.rem(gx + d, nx), gy, gz), None, None)
                    for d in range(1, nx)]

        def start(copies):
            for copy in copies:
                copy.start()

        def arrive(copies):
            for copy in copies:
                copy.arrive()

        srcs = (rhs, coef, s["sol"])
        P0 = [plane0(n, srcs[n]) for n in range(3)]
        Z0 = [z_halo(s["ext0"], n, R0) for n in range(3)]
        P1 = [plane1(n, n == 0) for n in range(3)]
        Z1 = [z_halo(s["ext1"], n, R1) for n in range(3)]
        Z2 = [z2(n) for n in range(3)]
        Y2 = [y2line(n) for n in range(3)]
        X2 = [x2line(n) for n in range(3)]

        def clear(dx, dy, dz, dsts):
            @pl.when(jnp.logical_not(has(dx, dy, dz)))
            def _():
                for ref, index in dsts:
                    ref[index] = jnp.zeros(ref.at[index].shape, F32)

        for dx, dy in DIRS:
            a, b = (0 if dx < 0 else 1), (0 if dy < 0 else 1)
            d = 1 + DIRS.index((dx, dy))
            dsts = []
            for n in range(3):
                if dy == 0:
                    dsts.append((s["xs0"], (n, a)))
                elif dx == 0:
                    dsts.append((s["ys0"], (n, b)))
                else:
                    dsts.append((s["ds0"], (n, 2 * a + b)))
                dsts.append((s["nat1"], (n, slice(4 * d, 4 * d + 4))))
            clear(dx, dy, 0, dsts)
        for e, (dx, dy) in enumerate(FAR):
            clear(dx, dy, 0, [(s["nat1"], (0, slice(36 + e, 37 + e)))])
        for dz in (-1, 1):
            dsts = []
            for n in range(3):
                dsts.append((s["ext0"], (n, slice(0, 8) if dz < 0 else slice(R0 - 8, R0))))
                dsts.append((s["ext1"], (n, slice(0, 8) if dz < 0 else slice(R1 - 8, R1))))
                dsts.append((s["zs2"], (n, 0 if dz < 0 else 1)))
            clear(0, 0, dz, dsts)
        s["nat1"][0, 42:48] = jnp.zeros((6, 8, 128), F32)
        for n in (1, 2):
            s["nat1"][n, 36:48] = jnp.zeros((12, 8, 128), F32)

        barrier = pltpu.get_barrier_semaphore()
        total = jnp.int32(nx - 1 + ny - 1)
        for d in range(1, nx):
            pl.semaphore_signal(barrier, inc=1, device_id=(lax.rem(gx + d, nx), gy, gz), device_id_type=MESH)
        for d in range(1, ny):
            pl.semaphore_signal(barrier, inc=1, device_id=(gx, lax.rem(gy + d, ny), gz), device_id_type=MESH)
        near = [(dx, dy, 0) for dx, dy in DIRS + FAR if dx and dy] + [(0, 0, -1), (0, 0, 1)]
        for dx, dy, dz in near:
            ok = has(dx, dy, dz)
            total = total + ok.astype(jnp.int32)

            @pl.when(ok)
            def _(dx=dx, dy=dy, dz=dz):
                pl.semaphore_signal(barrier, inc=1, device_id=(gx + dx, gy + dy, gz + dz), device_id_type=MESH)
        pl.semaphore_wait(barrier, total)

        start(P0[1])
        start(P0[0])

        k_nat = coef[...].reshape(128, 128)
        k1 = times(left(c["kx1"][...], k_nat), c["kz1"][...])
        s["nat1"][0, 0:4] = k1.reshape(4, 8, 128)
        start(P1[0])
        k2_half = left(c["kx2"][...], k_nat)
        k2_half = jnp.concatenate([k2_half, k2_half], axis=0)
        s["own2"][0] = times(k2_half, c["kz2"][...])[0:8]
        start(Z2[0])

        def shifts(v, xe):
            rows, lanes = v.shape
            return (pltpu.roll(v, lanes - 1, 1), pltpu.roll(v, 1, 1), pltpu.roll(v, lanes - xe, 1), pltpu.roll(v, xe, 1),
                    pltpu.roll(v, rows - 1, 0), pltpu.roll(v, 1, 0))

        def setup(k, xe, factor, inside, inner, extra, m, consts_ref):
            rows, lanes = k.shape
            ws = []
            for i, other in enumerate(shifts(k, xe)):
                if inner is not None and i < 4:
                    other = jnp.where(inner[i], other, 0.0)
                ws.append(0.5 * (k + other))
            diag = ws[0]
            for w in ws[1:]:
                diag = diag + w
            diag = factor * diag
            minv = jnp.where(inside, 0.8 / diag, 0.0)
            for i, w in enumerate(ws):
                link = (factor * minv) * w
                if inner is not None and i < 4:
                    link = jnp.where(inner[i], link, 0.0)
                if extra is not None:
                    link = jnp.where(extra[i], link, 0.0)
                m[i] = link
            consts_ref[0] = minv
            if consts_ref.shape[0] > 2:
                consts_ref[1] = 1.25 * diag

        def sweep(v, g, m, xe):
            total = 0.2 * v + g
            for i, other in enumerate(shifts(v, xe)):
                total = total + m[i] * other
            return total

        def coords(level, lanes, rows, x_off, y_off, z_off):
            x = c["coord"][2 * level:2 * level + 1, 0:lanes] + x_off
            y = c["coord"][2 * level + 1:2 * level + 2, 0:lanes] + y_off
            z = lax.broadcasted_iota(jnp.int32, (rows, lanes), 0) + z_off
            return x, y, z

        def inside_of(x, y, z, sizes):
            plane = (x >= 0) & (x < sizes[0]) & (y >= 0) & (y < sizes[1])
            return jnp.broadcast_to(plane, z.shape) & (z >= 0) & (z < sizes[2])

        def assemble0(n, own):
            blocks = [own, s["xs0"][n].reshape(128, 128), s["ys0"][n].reshape(128, 128), s["ds0"][n].reshape(128, 128)]
            wide = jnp.concatenate([b.T for b in blocks], axis=1)
            s["ext0"][n, 8:R0 - 8] = times(wide, c["place0"][...])

        def assemble1(n):
            nat = s["nat1"][n].reshape(384, 128)
            wide = jnp.concatenate([nat[128 * i:128 * i + 128].T for i in range(3)], axis=1)
            s["ext1"][n, 8:R1 - 8] = times(wide[0:64], c["place1"][...])

        def gather2_y(n):
            arrive(Z2[n])
            lane = lax.broadcasted_iota(jnp.int32, (8, 128), 1)
            both = jnp.where(lane < 32, s["zs2"][n, 0], jnp.where(lane < 64, s["own2"][n], s["zs2"][n, 1]))
            s["ys2"][n, gy] = both
            start(Y2[n])

        def gather2_x(n):
            arrive(Y2[n])
            start(X2[n])
            s["xs2"][n, gx] = s["ys2"][n]

        def gather2(n):
            arrive(X2[n])
            nat = s["xs2"][n].reshape(nx * ny * 8, 128)
            step = min(128, nat.shape[0])
            wide = jnp.concatenate([nat[i:i + step].T for i in range(0, nat.shape[0], step)], axis=1)
            return times(wide[0:R2], c["perm2"][...])

        arrive(P0[1])
        assemble0(1, k_nat)
        start(Z0[1])
        arrive(P0[0])
        assemble0(0, rhs[...].reshape(128, 128))
        start(Z0[0])
        gather2_y(0)
        arrive(P1[0])
        assemble1(0)
        start(Z1[0])

        x1, y1, z1 = coords(1, L1, R1, 4 * gx, 8 * gy, 64 * gz - 8)
        target = c["coord"][8:9, 0:L1] + (2 * gx + 4 * gy * x2)
        target = jnp.where((x1 >= 0) & (x1 < 4 * nx) & (y1 >= 0) & (y1 < 8 * ny), target, -1)
        s["prol1"][...] = jnp.where(lax.broadcasted_iota(jnp.int32, (l2, L1), 0) == target, 1.0, 0.0).astype(BF16)

        s["owners"][...] = jnp.dot(agg[...].astype(BF16), c["own3"][...], preferred_element_type=F32)

        arrive(Z0[1])
        x0, y0, z0 = coords(0, L0, R0, 8 * gx, 16 * gy, 128 * gz - 8)
        setup(s["ext0"][1], XE0, 1.0, inside_of(x0, y0, z0, (8 * nx, 16 * ny, 128 * nz)), None, None, s["m0"], s["c0"])
        arrive(Z0[0])
        s["c0"][2] = s["c0"][0] * s["ext0"][0]

        def halved(v, first, half):
            rows, lanes = v.shape
            sums = []
            for j in range(lanes // 128):
                s["pairs"][j, 0:rows] = v[:, 128 * j:128 * j + 128]
                sums.append(s["pairs"][j, pl.ds(first, half, stride=2), :] + s["pairs"][j, pl.ds(first + 1, half, stride=2), :])
            return sums[0] if len(sums) == 1 else jnp.concatenate(sums, axis=1)

        def doubled(v, first, rows):
            half, lanes = v.shape
            parts = []
            for j in range(lanes // 128):
                part = v[:, 128 * j:128 * j + 128]
                s["pairs"][j, pl.ds(0, half, stride=2), :] = part
                s["pairs"][j, pl.ds(1, half, stride=2), :] = part
                parts.append(s["pairs"][j, first:first + rows])
            return parts[0] if len(parts) == 1 else jnp.concatenate(parts, axis=1)

        def down(m, consts_ref, xe):
            g = consts_ref[2]
            v = sweep(g, g, m, xe)
            consts_ref[3] = v
            return v

        def residual(v, g, m, consts_ref, xe):
            return consts_ref[1] * (sweep(v, g, m, xe) - v)

        for cycle in range(2):
            n = 1 + cycle
            v = down(s["m0"], s["c0"], XE0)
            r = residual(v, s["c0"][2], s["m0"], s["c0"], XE0)
            s["nat1"][n, 0:4, :, 0:64] = select_t(c["sel0"][...], halved(r, 8, 64)).reshape(4, 8, 64)
            start(P1[n])
            if cycle == 0:
                gather2_x(0)
                arrive(Z1[0])
                inside = inside_of(x1, y1, z1, (4 * nx, 8 * ny, 64 * nz))
                setup(s["ext1"][0], XE1, 0.25, inside, None, None, s["m1"], s["c1"])
            arrive(P1[n])
            assemble1(n)
            start(Z1[n])
            arrive(Z1[n])
            s["c1"][2] = s["c1"][0] * s["ext1"][n]
            v = down(s["m1"], s["c1"], XE1)
            half = halved(residual(v, s["c1"][2], s["m1"], s["c1"], XE1), 8, 32)
            s["own2"][n, :, 0:96] = select_t(c["sel1"][...], jnp.concatenate([half, half, half], axis=0))
            start(Z2[n])
            if cycle == 0:
                k2 = gather2(0)
                x, y, z = coords(2, l2, R2, 0, 0, 32 * gz - 32)
                inner = [jnp.broadcast_to(q, z.shape) for q in (x + 1 < x2, x > 0, y + 1 < y2, y > 0)]
                setup(k2, x2, 0.0625, inside_of(x, y, z, (x2, y2, 32 * nz)), inner, None, s["m2"], s["c2"])
                k3 = times(halved(k2, 0, R3), c["rest2"][...])
                x, y, z = coords(3, l3, R3, 0, 0, 16 * gz - 16)
                inner = [jnp.broadcast_to(q, z.shape) for q in (x + 1 < nx, x > 0, y + 1 < 2 * ny, y > 0)]
                low, high = jnp.maximum(gz - 1, 0), jnp.minimum(gz + 1, nz - 1)
                owner = jnp.concatenate([jnp.broadcast_to(s["owners"][pl.ds(i, 1), :], (16, l3)) for i in (low, gz, high)], axis=0)
                same = [other == owner for other in shifts(owner, nx)]
                setup(k3, nx, 0.015625, inside_of(x, y, z, (nx, 2 * ny, 16 * nz)), inner, same, s["m3"], s["c3"])
            gather2_y(n)
            gather2_x(n)
            f2 = gather2(n)
            s["c2"][2] = s["c2"][0] * f2
            v2 = down(s["m2"], s["c2"], x2)
            r = residual(v2, s["c2"][2], s["m2"], s["c2"], x2)
            g3 = s["c3"][0] * times(halved(r, 0, R3), c["rest2"][...])
            e = g3
            for j in range(COARSE_SWEEPS - 1):
                e = sweep(e, g3, s["m3"], nx)
            fine = times(e, c["prol2"][...])
            v = s["c2"][3] + doubled(fine, 0, R2)
            for j in range(2):
                v = sweep(v, s["c2"][2], s["m2"], x2)
            fine = times(v[24:72], s["prol1"][...])
            v = s["c1"][3] + doubled(fine, 8, R1)
            for j in range(2):
                v = sweep(v, s["c1"][2], s["m1"], XE1)
            fine = times(v, c["prol0"][...])
            v = s["c0"][3] + doubled(fine, 8, R0)
            for j in range(2):
                v = sweep(v, s["c0"][2], s["m0"], XE0)
            nat = select_t(c["unsel"][...], v[8:R0 - 8])
            if cycle == 0:
                s["sol"][...] = nat.reshape(8, 16, 128)
                start(P0[2])
                arrive(P0[2])
                assemble0(2, nat)
                start(Z0[2])
                arrive(Z0[2])
                now = s["ext0"][2]
                s["c0"][2] = sweep(now, s["c0"][0] * s["ext0"][0], s["m0"], XE0) - now
            else:
                out[...] = s["sol"][...] + nat.reshape(8, 16, 128)
        for copy in unsent:
            copy.sent()

    vmem = pl.BlockSpec(memory_space=pltpu.VMEM)

    def body(rhs, coef, agglom):
        agg = jnp.zeros((8, 128), F32).at[:nz, :nx * ny].set(agglom.reshape(nx * ny, nz).T.astype(F32))
        return pl.pallas_call(
            kernel,
            out_shape=jax.ShapeDtypeStruct((8, 16, 128), F32),
            in_specs=[vmem] * (3 + len(names)),
            out_specs=vmem,
            scratch_shapes=[scratch[k] for k in keys],
            compiler_params=pltpu.CompilerParams(collective_id=0, has_side_effects=True, vmem_limit_bytes=60 * 1024 * 1024),
        )(rhs, coef, agg, *[jnp.asarray(consts[k]) for k in names])

    return body


def solution(mesh):
    body = build(mesh.shape["gx"], mesh.shape["gy"], mesh.shape["gz"])
    spec = P("gx", "gy", "gz")
    return jax.shard_map(body, mesh=mesh, in_specs=(spec, spec, P()), out_specs=spec, check_vma=False)
```

time: 1020 us -> 86 us (0.08); the launches traced: 1010 us -> 85.8 us
  starting transfers between devices: 490 us -> 0 us
  blocking collectives: 254 us -> 0 us
  waiting for transfers between devices: 193 us -> 0 us
  Pallas kernels: 0 us -> 81.6 us
  local copies, waits for them, and re-layouts: 26.5 us -> 2.23 us
  matrix products: 20.7 us -> 0 us
  other arithmetic: 15.7 us -> 1.98 us
    ppermute x174 -> x0, starting transfers between devices: 490 us -> none  [the longest x87 354 us: padded_2(): before = lax.ppermute(last, axis, up)]
    all_gather x4 -> x0, blocking collectives: 254 us -> none  [the longest x2 155 us: coarse_correct(): lax.all_gather(jnp.concatenate((flat, coarse_weights), axis=1), ('gx', 'g...]
    ppermute x174 -> x0, waiting for transfers between devices: 193 us -> none  [the longest x87 161 us: padded_2(): after = lax.ppermute(leading, axis, down)]
    pallas_call x0 -> x1, Pallas kernels: none -> 81.6 us  [body(): pl.pallas_call(kernel, out_shape=jax.ShapeDtypeStruct((8, 16, 128), F32),...]
    dot_general x88 -> x0, matrix products: 20.7 us -> none  [the longest x84 17.4 us: linked_values(): jnp.dot(links, errors.reshape(count, -1), precision=UPPER_LIMIT)]
    reshape x13 -> x0, local copies, waits for them, and re-layouts: 19.3 us -> none  [the longest x5 18.4 us: restrict(): return field.reshape(a // 2, 2, b // 2, 2, c // 2, 2).mean(axis=(1, 3, 5))]
    reduce_sum x17 -> x0, other arithmetic: 10.6 us -> none  [the longest x12 8.51 us: restrict(): return field.reshape(a // 2, 2, b // 2, 2, c // 2, 2).mean(axis=(1, 3, 5))]
  transfers between devices with their start and end apart: 174 -> 0, of which waited for: 81 -> 0; matrix products, arithmetic and copies ran while one was open for 1% -> 0% of each run, Pallas kernels for 0% -> 0%
where the time goes in v1:
time: 86 us; the launch traced here: 85.8 us
  Pallas kernels  81.6 us (95%)
  local copies, waits for them, and re-layouts  2.23 us (3%)
  other arithmetic  1.98 us (2%)
    pallas_call x1, Pallas kernels, body(): pl.pallas_call(kernel, out_shape=jax.ShapeDtypeStruct((8, 16, 128), F32),...  81.6 us
    another operation x2, other arithmetic  1.98 us

profile of v1, /device:TPU:1, one launch (start us, length us, event | category | flops | bytes accessed | tf_op | source)
XLA Modules:
  0.0 85.8 jit_solution(15387905836142511366)
XLA Ops:
  0.0 0.6 compare_reduce_fusion
  0.6 1.3 %fusion = f32[512]{0:T(512)S(1)} fusion(pred[]{:T(512)} %compare_reduce_fusion, s32[512,1]{0,1:T(1,128)} %param.22), kind=kLoop, calls=%fused_computation.1 | loop fusion | flops 1024 | bytes 4097 | tf_op jit(solution)/shard_map/select.3
  2.0 0.1 reshape.33
  2.1 0.1 copy.19
  2.1 0.6 scatter.4.agg
  2.8 81.6 %shard_map.172 = f32[8,16,128]{2,1,0:T(8,128)} custom-call(f32[8,16,128]{2,1,0:T(8,128)} %rhs.5, f32[8,16,128]{2,1,0:T(8,128)} %coef.1, f32[8,128]{1,0:T(8,128)} %scatter.4.agg, bf16[512,384]{1,0:T(8,128)(2,1)} %constant.61.clone.rest_0_, bf16[32,384]{1,0:T(8,128)(2,1)} %constant.62.clone.rest_1_, bf16[128,384]{1,0:T(8,128)(2,1)} %constant.63.clone.rest_2_, ...), custom_call_target="tpu_custom_call" | custom-call | tf_op jit(solution)/shard_map/pallas_call | solution.py:549
  84.3 1.5 %copy.21 = f32[8,16,128]{2,1,0:T(8,128)} copy(f32[8,16,128]{2,1,0:T(8,128)} %shard_map.172) | data formatting | bytes 131072

commit v2 on v1

v2 whole, which is shorter than its diff:
```python
import jax
import jax.numpy as jnp
import numpy as np
from jax import lax
from jax.experimental import pallas as pl
from jax.experimental.pallas import tpu as pltpu
from jax.sharding import PartitionSpec as P

F32 = jnp.float32
BF16 = jnp.bfloat16
MESH = pl.DeviceIdType.MESH
OUT = -100000
COARSE_SWEEPS = 8
DIRS = [(dx, dy) for dx in (-1, 0, 1) for dy in (-1, 0, 1) if (dx, dy) != (0, 0)]
ALL = [(0, 0)] + DIRS
FAR = [(dx, dy) for dx in (-2, 2) for dy in (-1, 0, 1)]
XE0, YE0, H0 = 16, 24, 4
XE1, YE1, H1 = 14, 18, 5
L0, L1 = 384, 256
R0, R1, R2, R3 = 144, 80, 96, 48


def up128(n):
    return -(-n // 128) * 128


def lane0(x, y):
    return (y + H0) * XE0 + x + H0


def lane1(x, y):
    return (y + H1) * XE1 + x + H1


def tables(nx, ny, nz):
    x2, y2 = 2 * nx, 4 * ny
    l2, l3 = up128(x2 * y2), up128(nx * 2 * ny)
    t = {}
    place0 = np.zeros((512, L0), np.float32)
    sel0 = np.zeros((32, L0), np.float32)
    unsel = np.zeros((128, L0), np.float32)
    for x in range(8):
        for y in range(16):
            place0[x * 16 + y, lane0(x, y)] = 1
            unsel[x * 16 + y, lane0(x, y)] = 1
            sel0[(x // 2) * 8 + y // 2, lane0(x, y)] = 0.125
    for x in range(8):
        for y in range(16):
            xx, yy = (x + 8 if x < 4 else x - 8), (y + 16 if y < 8 else y - 16)
            place0[128 + x * 16 + y, lane0(xx, y)] = 1
            if -H0 <= yy < 16 + H0:
                place0[256 + x * 16 + y, lane0(x, yy)] = 1
                place0[384 + x * 16 + y, lane0(xx, yy)] = 1
    place1 = np.zeros((384, L1), np.float32)
    for d, (sx, sy) in enumerate([(0, 0)] + DIRS):
        for x in range(4):
            for y in range(8):
                xx, yy = x + 4 * sx, y + 8 * sy
                if -H1 <= xx < 4 + H1 and -H1 <= yy < 8 + H1:
                    place1[32 * d + x * 8 + y, lane1(xx, yy)] = 1
    for e, (sx, sy) in enumerate(FAR):
        for y in range(8):
            xx, yy = (-5 if sx < 0 else 8), y + 8 * sy
            if -H1 <= yy < 8 + H1:
                place1[288 + 8 * e + y, lane1(xx, yy)] = 1
    sel1 = np.zeros((8, L1), np.float32)
    quarter = np.zeros((8, L1), np.float32)
    for x in range(4):
        for y in range(8):
            sel1[x // 2, lane1(x, y)] = 0.125
            quarter[y // 2, lane1(x, y)] = 1
    prol0 = np.zeros((L1, L0), np.float32)
    for x in range(-H0, 8 + H0):
        for y in range(-H0, 16 + H0):
            prol0[lane1(x // 2, y // 2), lane0(x, y)] = 1
    perm2 = np.zeros((nx * ny * 8, l2), np.float32)
    for a in range(nx):
        for b in range(ny):
            for i in range(2):
                for j in range(4):
                    perm2[j * nx * ny * 2 + (a * ny + b) * 2 + i, (b * 4 + j) * x2 + a * 2 + i] = 1
    rest2 = np.zeros((l2, l3), np.float32)
    for x in range(x2):
        for y in range(y2):
            rest2[y * x2 + x, (y // 2) * nx + x // 2] = 0.125
    prol2 = (rest2.T != 0).astype(np.float32)
    kx1 = np.zeros((32, 128), np.float32)
    kx2 = np.zeros((4, 8, 128), np.float32)
    for x in range(8):
        for y in range(16):
            kx1[(x // 2) * 8 + y // 2, x * 16 + y] = 0.25
            kx2[y // 4, x // 4, x * 16 + y] = 0.0625
    kz1 = np.zeros((128, 128), np.float32)
    kz2 = np.zeros((128, 128), np.float32)
    for z in range(128):
        kz1[z, z // 2] = 0.5
        for c in range(4):
            kz2[z, 32 * c + z // 4] = 0.25
    coord = np.full((16, max(L0, l2)), OUT, np.int32)
    for x in range(-H0, 8 + H0):
        for y in range(-H0, 16 + H0):
            coord[0:2, lane0(x, y)] = x, y
    for x in range(-H1, 4 + H1):
        for y in range(-H1, 8 + H1):
            coord[2:4, lane1(x, y)] = x, y
            coord[8, lane1(x, y)] = (y // 2) * x2 + x // 2
    for x in range(x2):
        for y in range(y2):
            coord[4:6, y * x2 + x] = x, y
    for x in range(nx):
        for y in range(2 * ny):
            coord[6:8, y * nx + x] = x, y
            coord[9, y * nx + x] = (x % 2) * ny * nz + (y // 2) * nz
    coord[10:14, 0:L1] = quarter[0:4]
    sel0r = np.concatenate([sel0] * 4, axis=0).T
    names = dict(sel0r=sel0r, place0=place0, sel0=sel0, unsel=unsel, place1=place1, sel1=sel1, prol0=prol0, perm2=perm2, rest2=rest2,
                 prol2=prol2, kx1=kx1, kx2=kx2.reshape(32, 128), kz1=kz1, kz2=kz2)
    t = {k: v.astype(jnp.bfloat16) for k, v in names.items()}
    t["coord"] = coord
    return t


def split(x):
    hi = x.astype(BF16)
    return hi, (x - hi.astype(F32)).astype(BF16)


def times(x, w):
    rows = x.shape[0]
    both = jnp.dot(jnp.concatenate(split(x), axis=0), w, preferred_element_type=F32)
    return both[:rows] + both[rows:]


def select_t(w, x):
    dims = (((1,), (1,)), ((), ()))
    hi, lo = split(x)
    return lax.dot_general(w, hi, dims, preferred_element_type=F32) + lax.dot_general(w, lo, dims, preferred_element_type=F32)


def left(w, x):
    hi, lo = split(x)
    return jnp.dot(w, hi, preferred_element_type=F32) + jnp.dot(w, lo, preferred_element_type=F32)


def build(nx, ny, nz):
    x2, y2 = 2 * nx, 4 * ny
    l2, l3 = up128(x2 * y2), up128(nx * 2 * ny)
    consts = tables(nx, ny, nz)
    names = list(consts)

    n_sem = 3 * 26 + 16 + 2 * 26 + 3 * (3 * ny + nx)

    scratch = dict(
        nat0=pltpu.VMEM((3, 3, 8, 16, 128), F32),
        slab0=pltpu.VMEM((3, 2, 8, 128), F32),
        slabs0=pltpu.VMEM((3, 2, 9, 8, 128), F32),
        rhs0=pltpu.VMEM((R0, L0), F32),
        nat1=pltpu.VMEM((3, 48, 8, 128), F32),
        slab1=pltpu.VMEM((3, 2, 8, 128), F32),
        slabs1=pltpu.VMEM((3, 2, 9, 8, 128), F32),
        ext1=pltpu.VMEM((R1, L1), F32),
        yz2=pltpu.VMEM((3, 3, ny, 2, 128), F32),
        xs2=pltpu.VMEM((3, nx, 3, ny, 2, 128), F32),
        rhs_v=pltpu.VMEM((8, 16, 128), F32),
        coef_v=pltpu.VMEM((8, 16, 128), F32),
        sol=pltpu.VMEM((8, 16, 128), F32),
        m0=pltpu.VMEM((6, R0, L0), F32),
        c0=pltpu.VMEM((4, R0, L0), F32),
        m1=pltpu.VMEM((6, R1, L1), F32),
        c1=pltpu.VMEM((4, R1, L1), F32),
        m2=pltpu.VMEM((6, R2, l2), F32),
        c2=pltpu.VMEM((4, R2, l2), F32),
        m3=pltpu.VMEM((6, R3, l3), F32),
        c3=pltpu.VMEM((2, R3, l3), F32),
        pairs=pltpu.VMEM((max(L0, l2) // 128, 160, 128), F32),
        prol1=pltpu.VMEM((l2, L1), BF16),
        lsem=pltpu.SemaphoreType.DMA((2 + len(names),)),
        ssem=pltpu.SemaphoreType.DMA((n_sem,)),
        rsem=pltpu.SemaphoreType.DMA((n_sem,)),
    )
    keys = list(scratch)
    held = [pltpu.VMEM(consts[k].shape, consts[k].dtype) for k in names]

    def kernel(rhs_hbm, coef_hbm, agg, *rest):
        out = rest[len(names)]
        s = dict(zip(keys, rest[len(names) + 1:]))
        local = dict(zip(names, rest[len(names) + 1 + len(keys):]))
        rhs, coef = s["rhs_v"], s["coef_v"]
        loads = {"rhs": pltpu.make_async_copy(rhs_hbm, rhs, s["lsem"].at[0]), "coef": pltpu.make_async_copy(coef_hbm, coef, s["lsem"].at[1])}
        for i, k in enumerate(names):
            loads[k] = pltpu.make_async_copy(rest[i], local[k], s["lsem"].at[2 + i])
        waited = set()

        def ready(k):
            if k not in waited:
                waited.add(k)
                loads[k].wait()

        class Table:
            def __getitem__(self, k):
                ready(k)
                return local[k]

        c = Table()
        gx, gy, gz = lax.axis_index("gx"), lax.axis_index("gy"), lax.axis_index("gz")

        def has(dx, dy, dz):
            ok = None
            for g, d, n in ((gx, dx, nx), (gy, dy, ny), (gz, dz, nz)):
                if d:
                    here = (g + d >= 0) if d < 0 else (g + d < n)
                    ok = here if ok is None else ok & here
            return ok

        counter = [0]
        unsent = []

        class Copy:
            def __init__(self, src, dst, there, send_if, recv_if):
                i = counter[0]
                counter[0] += 1
                self.make = lambda: pltpu.make_async_remote_copy(
                    src_ref=src, dst_ref=dst, send_sem=s["ssem"].at[i], recv_sem=s["rsem"].at[i],
                    device_id=there, device_id_type=MESH)
                self.send_if, self.recv_if = send_if, recv_if
                unsent.append(self)
                self.started = False

            def under(self, cond, f):
                if cond is None:
                    f()
                else:
                    pl.when(cond)(f)

            def start(self):
                self.started = True
                self.under(self.send_if, lambda: self.make().start())

            def arrive(self):
                self.under(self.recv_if, lambda: self.make().wait_recv())

            def sent(self):
                self.under(self.send_if, lambda: self.make().wait_send())

        def toward(dx, dy, dz, src, dst):
            return Copy(src, dst, (gx + dx, gy + dy, gz + dz), has(dx, dy, dz), has(-dx, -dy, -dz))

        def halo0(n, src):
            copies = []
            for dx, dy in DIRS:
                xs = slice(0, 8) if dx == 0 else (slice(4, 8) if dx > 0 else slice(0, 4))
                ys = slice(0, 16) if dy == 0 else (slice(8, 16) if dy > 0 else slice(0, 8))
                group = 0 if dy == 0 else (1 if dx == 0 else 2)
                copies.append(toward(dx, dy, 0, src.at[xs, ys, :], s["nat0"].at[n, group, xs, ys, :]))
            return copies

        def slab_halo(n, slab, slabs):
            return [toward(dx, dy, dz, slab.at[n, 0 if dz < 0 else 1], slabs.at[n, 1 if dz < 0 else 0, ALL.index((-dx, -dy))])
                    for dx, dy in reversed(ALL) for dz in (-1, 1)]

        def plane1(n):
            copies = []
            for dx, dy in DIRS:
                d = ALL.index((-dx, -dy))
                copies.append(toward(dx, dy, 0, s["nat1"].at[n, 0:4], s["nat1"].at[n, 4 * d:4 * d + 4]))
            return copies

        def far1(n):
            copies = []
            for dx, dy in FAR:
                e = FAR.index((-dx, -dy))
                i = 3 if dx > 0 else 0
                copies.append(toward(dx, dy, 0, s["nat1"].at[n, i:i + 1], s["nat1"].at[n, 36 + e:37 + e]))
            return copies

        def z_halo1():
            return [toward(0, 0, -1, s["ext1"].at[8:16, :], s["ext1"].at[R1 - 8:R1, :]),
                    toward(0, 0, 1, s["ext1"].at[R1 - 16:R1 - 8, :], s["ext1"].at[0:8, :])]

        def yzline(n):
            mine = s["yz2"].at[n, 1, gy]
            return [Copy(mine, s["yz2"].at[n, 1 - dz, gy], (gx, lax.rem(gy + d, ny), gz + dz), has(0, 0, dz), has(0, 0, -dz))
                    for d in sorted(range(ny), key=lambda d: -min(d, ny - d)) for dz in (-1, 1, 0) if d or dz]

        def xline(n):
            return [Copy(s["yz2"].at[n], s["xs2"].at[n, gx], (lax.rem(gx + d, nx), gy, gz), None, None)
                    for d in sorted(range(1, nx), key=lambda d: -min(d, nx - d))]

        def start(copies):
            for copy in copies:
                copy.start()

        def arrive(copies):
            done = [copy for copy in unsent if copy.started and copy not in copies]
            for copy in done:
                copy.sent()
                unsent.remove(copy)
            for copy in copies:
                copy.arrive()

        srcs = (rhs, coef, s["sol"])
        srcs = (rhs, coef, s["sol"])
        P0 = [halo0(n, srcs[n]) for n in range(3)]
        S0 = [slab_halo(n, s["slab0"], s["slabs0"]) for n in range(3)]
        P1 = [plane1(n) for n in range(3)]
        S1 = [None] + [slab_halo(n, s["slab1"], s["slabs1"]) for n in (1, 2)]
        F1 = far1(0)
        Z1 = z_halo1()
        Y2 = [yzline(n) for n in range(3)]
        X2 = [xline(n) for n in range(3)]

        barrier = pltpu.get_barrier_semaphore()
        for d in range(1, nx):
            pl.semaphore_signal(barrier, inc=1, device_id=(lax.rem(gx + d, nx), gy, gz), device_id_type=MESH)
        for d in range(1, ny):
            pl.semaphore_signal(barrier, inc=1, device_id=(gx, lax.rem(gy + d, ny), gz), device_id_type=MESH)
        total = jnp.int32(nx - 1 + ny - 1)
        for dz in (-1, 1):
            ok = has(0, 0, dz)
            total = total + ny * ok.astype(jnp.int32)

            @pl.when(ok)
            def _(dz=dz):
                for d in range(ny):
                    pl.semaphore_signal(barrier, inc=1, device_id=(gx, lax.rem(gy + d, ny), gz + dz), device_id_type=MESH)
        near = [(dx, dy, 0) for dx, dy in DIRS + FAR if dx and dy] + [(dx, dy, dz) for dx, dy in DIRS if dx for dz in (-1, 1)]
        for dx, dy, dz in near:
            ok = has(dx, dy, dz)
            total = total + ok.astype(jnp.int32)

            @pl.when(ok)
            def _(dx=dx, dy=dy, dz=dz):
                pl.semaphore_signal(barrier, inc=1, device_id=(gx + dx, gy + dy, gz + dz), device_id_type=MESH)

        for k in ["coef", "rhs", "kx1", "kx2", "kz1", "kz2", "place0"]:
            loads[k].start()
        for k in names:
            if k not in ("kx1", "kx2", "kz1", "kz2", "place0"):
                loads[k].start()

        def clear(dx, dy, dz, dsts):
            @pl.when(jnp.logical_not(has(dx, dy, dz)))
            def _():
                for ref, index in dsts:
                    ref[index] = jnp.zeros(ref.at[index].shape, F32)

        for dx, dy in DIRS:
            xs = slice(0, 8) if dx == 0 else (slice(4, 8) if dx < 0 else slice(0, 4))
            ys = slice(0, 16) if dy == 0 else (slice(8, 16) if dy < 0 else slice(0, 8))
            group = 0 if dy == 0 else (1 if dx == 0 else 2)
            d = ALL.index((dx, dy))
            dsts = []
            for n in range(3):
                dsts.append((s["nat0"], (n, group, xs, ys)))
                dsts.append((s["nat1"], (n, slice(4 * d, 4 * d + 4))))
                for side in range(2):
                    dsts.append((s["slabs0"], (n, side, d)))
                    if n:
                        dsts.append((s["slabs1"], (n, side, d)))
            clear(dx, dy, 0, dsts)
        for e, (dx, dy) in enumerate(FAR):
            clear(dx, dy, 0, [(s["nat1"], (0, slice(36 + e, 37 + e)))])
        for dz in (-1, 1):
            side = 0 if dz < 0 else 1
            dsts = [(s["ext1"], (slice(0, 8) if dz < 0 else slice(R1 - 8, R1),))]
            for n in range(3):
                dsts.append((s["slabs0"], (n, side)))
                if n:
                    dsts.append((s["slabs1"], (n, side)))
                dsts.append((s["yz2"], (n, 1 + dz)))
            clear(0, 0, dz, dsts)
        s["nat1"][0, 42:48] = jnp.zeros((6, 8, 128), F32)
        for n in (1, 2):
            s["nat1"][n, 36:48] = jnp.zeros((12, 8, 128), F32)

        ready("coef")
        k_nat = coef[...].reshape(128, 128)
        k_flip = k_nat.T
        s["slab0"][1, 0] = k_flip[0:8]
        s["slab0"][1, 1] = k_flip[120:128]
        ready("rhs")
        f_flip = rhs[...].reshape(128, 128).T
        s["slab0"][0, 0] = f_flip[0:8]
        s["slab0"][0, 1] = f_flip[120:128]
        pl.semaphore_wait(barrier, total)
        start(S0[1])
        start(P0[1])
        start(S0[0])
        start(P0[0])
        k1 = times(left(c["kx1"][...], k_nat), c["kz1"][...])
        s["nat1"][0, 0:4] = k1.reshape(4, 8, 128)
        start(P1[0])
        start(F1)
        k2_parts = times(left(c["kx2"][...], k_nat), c["kz2"][...])
        lane = lax.broadcasted_iota(jnp.int32, (8, 128), 1)

        def by_quarter(parts):
            return jnp.where(lane < 32, parts[0], jnp.where(lane < 64, parts[1], jnp.where(lane < 96, parts[2], parts[3])))

        s["yz2"][0, 1, gy] = by_quarter([k2_parts[8 * q:8 * q + 8] for q in range(4)])[0:2]
        start(Y2[0])

        def shifts(v, xe):
            rows, lanes = v.shape
            return (pltpu.roll(v, lanes - 1, 1), pltpu.roll(v, 1, 1), pltpu.roll(v, lanes - xe, 1), pltpu.roll(v, xe, 1),
                    pltpu.roll(v, rows - 1, 0), pltpu.roll(v, 1, 0))

        def setup(k, xe, factor, inside, inner, extra, m, consts_ref):
            rows, lanes = k.shape
            ws = []
            for i, other in enumerate(shifts(k, xe)):
                if inner is not None and i < 4:
                    other = jnp.where(inner[i], other, 0.0)
                ws.append(0.5 * (k + other))
            diag = ws[0]
            for w in ws[1:]:
                diag = diag + w
            diag = factor * diag
            minv = jnp.where(inside, 0.8 / diag, 0.0)
            for i, w in enumerate(ws):
                link = (factor * minv) * w
                if inner is not None and i < 4:
                    link = jnp.where(inner[i], link, 0.0)
                if extra is not None:
                    link = jnp.where(extra[i], link, 0.0)
                m[i] = link
            consts_ref[0] = minv
            if consts_ref.shape[0] > 2:
                consts_ref[1] = 1.25 * diag

        def sweep(v, g, m, xe):
            total = 0.2 * v + g
            for i, other in enumerate(shifts(v, xe)):
                total = total + m[i] * other
            return total

        def coords(level, lanes, rows, x_off, y_off, z_off):
            x = c["coord"][2 * level:2 * level + 1, 0:lanes] + x_off
            y = c["coord"][2 * level + 1:2 * level + 2, 0:lanes] + y_off
            z = lax.broadcasted_iota(jnp.int32, (rows, lanes), 0) + z_off
            return x, y, z

        def inside_of(x, y, z, sizes):
            plane = (x >= 0) & (x < sizes[0]) & (y >= 0) & (y < sizes[1])
            return jnp.broadcast_to(plane, z.shape) & (z >= 0) & (z < sizes[2])

        def assemble0(n, flipped):
            blocks = [flipped] + [s["nat0"][n, i].reshape(128, 128).T for i in range(3)]
            right = lane < 64
            above = lax.rem(lane, 16) < 8
            ends = []
            for side in range(2):
                def at(dx, dy, side=side):
                    return s["slabs0"][n, side, ALL.index((dx, dy))]

                ends.append(jnp.concatenate([
                    at(0, 0), jnp.where(right, at(1, 0), at(-1, 0)), jnp.where(above, at(0, 1), at(0, -1)),
                    jnp.where(right, jnp.where(above, at(1, 1), at(1, -1)), jnp.where(above, at(-1, 1), at(-1, -1)))], axis=1))
            wide = jnp.concatenate([ends[0], jnp.concatenate(blocks, axis=1), ends[1]], axis=0)
            return times(wide, c["place0"][...])

        def natural1(n):
            nat = s["nat1"][n].reshape(384, 128)
            return jnp.concatenate([nat[128 * i:128 * i + 128].T for i in range(3)], axis=1)[0:64]

        def assemble1(n):
            ends = []
            for side in range(2):
                slabs = [s["slabs1"][n, side, d] for d in range(9)]
                ends.append(jnp.concatenate([by_quarter(slabs[0:4]), by_quarter(slabs[4:8]), jnp.where(lane < 32, slabs[8], 0.0)], axis=1))
            wide = jnp.concatenate([ends[0], natural1(n), ends[1]], axis=0)
            return times(wide, c["place1"][...])

        def gather2_x(n):
            arrive(Y2[n])
            start(X2[n])
            s["xs2"][n, gx] = s["yz2"][n]

        def gather2(n):
            arrive(X2[n])
            rows = []
            for dz in range(3):
                flipped = s["xs2"][n, :, dz].reshape(nx * ny * 2, 128).T
                rows.append(jnp.concatenate([flipped[32 * q:32 * q + 32] for q in range(4)], axis=1))
            return times(jnp.concatenate(rows, axis=0), c["perm2"][...])

        x1, y1, z1 = coords(1, L1, R1, 4 * gx, 8 * gy, 64 * gz - 8)
        target = c["coord"][8:9, 0:L1] + (2 * gx + 4 * gy * x2)
        target = jnp.where((x1 >= 0) & (x1 < 4 * nx) & (y1 >= 0) & (y1 < 8 * ny), target, -1)
        s["prol1"][...] = jnp.where(lax.broadcasted_iota(jnp.int32, (l2, L1), 0) == target, 1.0, 0.0).astype(BF16)

        near_owner = []
        xb = c["coord"][6:7, 0:l3]
        for i in (jnp.maximum(gz - 1, 0), gz, jnp.minimum(gz + 1, nz - 1)):
            pick = lax.broadcasted_iota(jnp.int32, (2 * ny * nz, l3), 0) == c["coord"][9:10, 0:l3] + i
            picked = jnp.dot(agg[...].astype(F32).astype(BF16), jnp.where(pick, 1.0, 0.0).astype(BF16), preferred_element_type=F32)
            mine = jnp.zeros((1, l3), F32)
            for r in range(nx // 2):
                mine = jnp.where(xb // 2 == r, picked[r:r + 1], mine)
            near_owner.append(jnp.broadcast_to(mine, (16, l3)))
        owner = jnp.concatenate(near_owner, axis=0)

        arrive(P1[0] + F1)
        s["ext1"][8:R1 - 8] = times(natural1(0), c["place1"][...])
        start(Z1)

        arrive(P0[1] + S0[1])
        k0 = assemble0(1, k_flip)
        x0, y0, z0 = coords(0, L0, R0, 8 * gx, 16 * gy, 128 * gz - 8)
        setup(k0, XE0, 1.0, inside_of(x0, y0, z0, (8 * nx, 16 * ny, 128 * nz)), None, None, s["m0"], s["c0"])
        arrive(P0[0] + S0[0])
        f0 = assemble0(0, f_flip)
        s["rhs0"][...] = f0
        s["c0"][2] = s["c0"][0] * f0

        def halved(v, first, half):
            rows, lanes = v.shape
            sums = []
            for j in range(lanes // 128):
                s["pairs"][j, 0:rows] = v[:, 128 * j:128 * j + 128]
                sums.append(s["pairs"][j, pl.ds(first, half, stride=2), :] + s["pairs"][j, pl.ds(first + 1, half, stride=2), :])
            return sums[0] if len(sums) == 1 else jnp.concatenate(sums, axis=1)

        def doubled(v, first, rows):
            half, lanes = v.shape
            parts = []
            for j in range(lanes // 128):
                part = v[:, 128 * j:128 * j + 128]
                s["pairs"][j, pl.ds(0, half, stride=2), :] = part
                s["pairs"][j, pl.ds(1, half, stride=2), :] = part
                parts.append(s["pairs"][j, first:first + rows])
            return parts[0] if len(parts) == 1 else jnp.concatenate(parts, axis=1)

        def down(m, consts_ref, xe):
            g = consts_ref[2]
            v = sweep(g, g, m, xe)
            consts_ref[3] = v
            return v

        def residual(v, g, m, consts_ref, xe):
            return consts_ref[1] * (sweep(v, g, m, xe) - v)

        for cycle in range(2):
            n = 1 + cycle
            v = down(s["m0"], s["c0"], XE0)
            r = residual(v, s["c0"][2], s["m0"], s["c0"], XE0)
            half = halved(r, 8, 64)
            ends = times(jnp.concatenate([half[0:8], half[56:64]], axis=0), c["sel0r"][...])
            s["slab1"][n] = ends.reshape(2, 8, 128)
            start(S1[n])
            s["nat1"][n, 0:4, :, 0:64] = select_t(c["sel0"][...], half).reshape(4, 8, 64)
            start(P1[n])
            if cycle == 0:
                gather2_x(0)
                arrive(Z1)
                inside = inside_of(x1, y1, z1, (4 * nx, 8 * ny, 64 * nz))
                setup(s["ext1"][...], XE1, 0.25, inside, None, None, s["m1"], s["c1"])
            arrive(P1[n] + S1[n])
            s["c1"][2] = s["c1"][0] * assemble1(n)
            v = down(s["m1"], s["c1"], XE1)
            half = halved(residual(v, s["c1"][2], s["m1"], s["c1"], XE1), 8, 32)
            quarters = [jnp.where(c["coord"][10 + q:11 + q, 0:L1] > 0, half, 0.0) for q in range(4)]
            s["yz2"][n, 1, gy] = select_t(c["sel1"][...], jnp.concatenate(quarters, axis=0))[0:2]
            start(Y2[n])
            if cycle == 0:
                k2 = gather2(0)
                x, y, z = coords(2, l2, R2, 0, 0, 32 * gz - 32)
                inner = [jnp.broadcast_to(q, z.shape) for q in (x + 1 < x2, x > 0, y + 1 < y2, y > 0)]
                setup(k2, x2, 0.0625, inside_of(x, y, z, (x2, y2, 32 * nz)), inner, None, s["m2"], s["c2"])
                k3 = times(halved(k2, 0, R3), c["rest2"][...])
                x, y, z = coords(3, l3, R3, 0, 0, 16 * gz - 16)
                inner = [jnp.broadcast_to(q, z.shape) for q in (x + 1 < nx, x > 0, y + 1 < 2 * ny, y > 0)]
                same = [other == owner for other in shifts(owner, nx)]
                setup(k3, nx, 0.015625, inside_of(x, y, z, (nx, 2 * ny, 16 * nz)), inner, same, s["m3"], s["c3"])
            gather2_x(n)
            f2 = gather2(n)
            s["c2"][2] = s["c2"][0] * f2
            v2 = down(s["m2"], s["c2"], x2)
            r = residual(v2, s["c2"][2], s["m2"], s["c2"], x2)
            g3 = s["c3"][0] * times(halved(r, 0, R3), c["rest2"][...])
            e = g3
            for j in range(COARSE_SWEEPS - 1):
                e = sweep(e, g3, s["m3"], nx)
            fine = times(e, c["prol2"][...])
            v = s["c2"][3] + doubled(fine, 0, R2)
            for j in range(2):
                v = sweep(v, s["c2"][2], s["m2"], x2)
            fine = times(v[24:72], s["prol1"][...])
            v = s["c1"][3] + doubled(fine, 8, R1)
            for j in range(2):
                v = sweep(v, s["c1"][2], s["m1"], XE1)
            fine = times(v, c["prol0"][...])
            v = s["c0"][3] + doubled(fine, 8, R0)
            for j in range(2):
                v = sweep(v, s["c0"][2], s["m0"], XE0)
            nat = select_t(c["unsel"][...], v[8:R0 - 8])
            if cycle == 0:
                s["sol"][...] = nat.reshape(8, 16, 128)
                flipped = nat.T
                s["slab0"][2, 0] = flipped[0:8]
                s["slab0"][2, 1] = flipped[120:128]
                start(S0[2])
                start(P0[2])
                arrive(P0[2] + S0[2])
                now = assemble0(2, flipped)
                s["c0"][2] = sweep(now, s["c0"][0] * s["rhs0"][...], s["m0"], XE0) - now
            else:
                out[...] = s["sol"][...] + nat.reshape(8, 16, 128)
        for k in loads:
            ready(k)
        for copy in unsent:
            copy.sent()

    vmem = pl.BlockSpec(memory_space=pltpu.VMEM)
    hbm = pl.BlockSpec(memory_space=pl.ANY)

    def body(rhs, coef, agglom):
        agg = agglom.reshape(nx // 2, 2 * ny * nz)
        return pl.pallas_call(
            kernel,
            out_shape=pltpu.VMEM((8, 16, 128), F32),
            in_specs=[hbm, hbm, vmem] + [hbm] * len(names),
            out_specs=vmem,
            scratch_shapes=[scratch[k] for k in keys] + held,
            compiler_params=pltpu.CompilerParams(collective_id=0, has_side_effects=True, vmem_limit_bytes=60 * 1024 * 1024),
        )(rhs, coef, agg, *[jnp.asarray(consts[k]) for k in names])

    return body


def solution(mesh):
    body = build(mesh.shape["gx"], mesh.shape["gy"], mesh.shape["gz"])
    spec = P("gx", "gy", "gz")
    return jax.shard_map(body, mesh=mesh, in_specs=(spec, spec, P()), out_specs=spec, check_vma=False)
```

time: 86 us -> 73.1 us (0.85)
  Pallas kernels: 81.6 us -> 72.3 us
  other arithmetic: 1.98 us -> 0 us
  local copies, waits for them, and re-layouts: 2.23 us -> 0.63 us
    pallas_call x1, Pallas kernels: 81.6 us -> 72.3 us  [body(): pl.pallas_call(kernel, out_shape=pltpu.VMEM((8, 16, 128), F32), in_specs=...]
    another operation x2 -> x0, other arithmetic: 1.98 us -> none
where the time goes in v2:
time: 73.1 us; the launch traced here: 73 us
  Pallas kernels  72.3 us (99%)
    pallas_call x1, Pallas kernels, body(): pl.pallas_call(kernel, out_shape=pltpu.VMEM((8, 16, 128), F32), in_specs=...  72.3 us

profile of v2, /device:TPU:1, one launch (start us, length us, event | category | flops | bytes accessed | tf_op | source)
XLA Modules:
  0.0 73.0 jit_solution(7899414199388717074)
XLA Ops:
  0.0 72.3 %shard_map.172 = f32[8,16,128]{2,1,0:T(8,128)S(1)} custom-call(f32[8,16,128]{2,1,0:T(8,128)} %rhs_hbm.1, f32[8,16,128]{2,1,0:T(8,128)} %coef_hbm.1, s32[4,128]{1,0:T(4,128)} %bitcast.1, bf16[384,128]{1,0:T(8,128)(2,1)} %constant.30.clone.rest_0_, bf16[512,384]{1,0:T(8,128)(2,1)} %constant.31.clone.rest_1_, bf16[32,384]{1,0:T(8,128)(2,1)} %constant.32.clone.rest_2_, ...), custom_call_target="tpu_custom_call" | custom-call | tf_op jit(solution)/shard_map/pallas_call | solution.py:619
  72.3 0.6 copy.20

commit v3 on v2

--- a/solution.py
+++ b/solution.py
@@ -36,7 +36,7 @@
     x2, y2 = 2 * nx, 4 * ny
     l2, l3 = up128(x2 * y2), up128(nx * 2 * ny)
     t = {}
-    place0 = np.zeros((512, L0), np.float32)
+    place0 = np.zeros((384, L0), np.float32)
     sel0 = np.zeros((32, L0), np.float32)
     unsel = np.zeros((128, L0), np.float32)
     for x in range(8):
@@ -46,11 +46,16 @@
             sel0[(x // 2) * 8 + y // 2, lane0(x, y)] = 0.125
     for x in range(8):
         for y in range(16):
-            xx, yy = (x + 8 if x < 4 else x - 8), (y + 16 if y < 8 else y - 16)
-            place0[128 + x * 16 + y, lane0(xx, y)] = 1
-            if -H0 <= yy < 16 + H0:
-                place0[256 + x * 16 + y, lane0(x, yy)] = 1
-                place0[384 + x * 16 + y, lane0(xx, yy)] = 1
+            place0[128 + x * 16 + y, lane0(x + 8 if x < 4 else x - 8, y)] = 1
+        for yi in range(H0):
+            place0[256 + x * 4 + yi, lane0(x, yi - H0)] = 1
+            place0[288 + x * 4 + yi, lane0(x, yi + 16)] = 1
+            if x >= 4:
+                place0[320 + (x - 4) * 4 + yi, lane0(x - 8, yi - H0)] = 1
+                place0[336 + (x - 4) * 4 + yi, lane0(x - 8, yi + 16)] = 1
+            else:
+                place0[352 + x * 4 + yi, lane0(x + 8, yi - H0)] = 1
+                place0[368 + x * 4 + yi, lane0(x + 8, yi + 16)] = 1
     place1 = np.zeros((384, L1), np.float32)
     for d, (sx, sy) in enumerate([(0, 0)] + DIRS):
         for x in range(4):
@@ -148,11 +153,13 @@
     consts = tables(nx, ny, nz)
     names = list(consts)
 
-    n_sem = 3 * 26 + 16 + 2 * 26 + 3 * (3 * ny + nx)
+    n_sem = 13
 
     scratch = dict(
-        nat0=pltpu.VMEM((3, 3, 8, 16, 128), F32),
-        slab0=pltpu.VMEM((3, 2, 8, 128), F32),
+        x0=pltpu.VMEM((3, 8, 16, 128), F32),
+        pack0=pltpu.VMEM((3, 8, 8, 128), F32),
+        y0=pltpu.VMEM((3, 16, 8, 128), F32),
+        slab0=pltpu.VMEM((3, 2, 2, 8, 128), F32),
         slabs0=pltpu.VMEM((3, 2, 9, 8, 128), F32),
         rhs0=pltpu.VMEM((R0, L0), F32),
         nat1=pltpu.VMEM((3, 48, 8, 128), F32),
@@ -161,9 +168,7 @@
         ext1=pltpu.VMEM((R1, L1), F32),
         yz2=pltpu.VMEM((3, 3, ny, 2, 128), F32),
         xs2=pltpu.VMEM((3, nx, 3, ny, 2, 128), F32),
-        rhs_v=pltpu.VMEM((8, 16, 128), F32),
-        coef_v=pltpu.VMEM((8, 16, 128), F32),
-        sol=pltpu.VMEM((8, 16, 128), F32),
+        cells=pltpu.VMEM((3, 8, 16, 128), F32),
         m0=pltpu.VMEM((6, R0, L0), F32),
         c0=pltpu.VMEM((4, R0, L0), F32),
         m1=pltpu.VMEM((6, R1, L1), F32),
@@ -173,32 +178,43 @@
         m3=pltpu.VMEM((6, R3, l3), F32),
         c3=pltpu.VMEM((2, R3, l3), F32),
         pairs=pltpu.VMEM((max(L0, l2) // 128, 160, 128), F32),
+        agg=pltpu.VMEM((nx // 2, 2 * ny * nz), jnp.int32),
         prol1=pltpu.VMEM((l2, L1), BF16),
-        lsem=pltpu.SemaphoreType.DMA((2 + len(names),)),
+        zero16=pltpu.VMEM((2, 4, 16, 128), F32),
+        zero8=pltpu.VMEM((2, 4, 8, 128), F32),
+        zero2=pltpu.VMEM((2, 128), F32),
+        zero_w=pltpu.VMEM((8, L1), F32),
+        void8=pltpu.VMEM((104, 8, 128), F32),
+        void2=pltpu.VMEM((max(nx, 2) * 3 * ny, 2, 128), F32),
+        lsem=pltpu.SemaphoreType.DMA((4,)),
         ssem=pltpu.SemaphoreType.DMA((n_sem,)),
         rsem=pltpu.SemaphoreType.DMA((n_sem,)),
     )
     keys = list(scratch)
     held = [pltpu.VMEM(consts[k].shape, consts[k].dtype) for k in names]
 
-    def kernel(rhs_hbm, coef_hbm, agg, *rest):
+    def kernel(rhs_hbm, coef_hbm, agg_hbm, *rest):
         out = rest[len(names)]
         s = dict(zip(keys, rest[len(names) + 1:]))
         local = dict(zip(names, rest[len(names) + 1 + len(keys):]))
-        rhs, coef = s["rhs_v"], s["coef_v"]
-        loads = {"rhs": pltpu.make_async_copy(rhs_hbm, rhs, s["lsem"].at[0]), "coef": pltpu.make_async_copy(coef_hbm, coef, s["lsem"].at[1])}
-        for i, k in enumerate(names):
-            loads[k] = pltpu.make_async_copy(rest[i], local[k], s["lsem"].at[2 + i])
+        rhs, coef = s["cells"].at[0], s["cells"].at[1]
+        early = ["kx1", "kx2", "kz1", "kz2", "coord"]
+        late = [k for k in names if k not in early]
+        sources = dict(zip(names, rest))
+        loads = {"rhs": [(rhs_hbm, rhs)], "coef": [(coef_hbm, coef)],
+                 "early": [(sources[k], local[k]) for k in early] + [(agg_hbm, s["agg"])], "late": [(sources[k], local[k]) for k in late]}
+        loads = {k: [pltpu.make_async_copy(a, b, s["lsem"].at[i]) for a, b in pairs] for i, (k, pairs) in enumerate(loads.items())}
         waited = set()
 
         def ready(k):
             if k not in waited:
                 waited.add(k)
-                loads[k].wait()
+                for load in loads[k]:
+                    load.wait()
 
         class Table:
             def __getitem__(self, k):
-                ready(k)
+                ready("early" if k in early else "late")
                 return local[k]
 
         c = Table()
@@ -212,57 +228,79 @@
                     ok = here if ok is None else ok & here
             return ok
 
-        counter = [0]
-        unsent = []
+        stages = [0]
+        absent = {}
 
         class Copy:
-            def __init__(self, src, dst, there, send_if, recv_if):
-                i = counter[0]
-                counter[0] += 1
+            def __init__(self, src, dst, there, send_if):
+                i = stages[0]
                 self.make = lambda: pltpu.make_async_remote_copy(
                     src_ref=src, dst_ref=dst, send_sem=s["ssem"].at[i], recv_sem=s["rsem"].at[i],
                     device_id=there, device_id_type=MESH)
-                self.send_if, self.recv_if = send_if, recv_if
-                unsent.append(self)
-                self.started = False
-
-            def under(self, cond, f):
-                if cond is None:
+                self.send_if = send_if
+
+            def under(self, f):
+                if self.send_if is None:
                     f()
                 else:
-                    pl.when(cond)(f)
+                    pl.when(self.send_if)(f)
 
             def start(self):
-                self.started = True
-                self.under(self.send_if, lambda: self.make().start())
+                self.under(lambda: self.make().start())
+
+            def sent(self):
+                self.under(lambda: self.make().wait_send())
+
+        def toward(dx, dy, dz, src, dst, zero):
+            i = stages[0]
+            absent.setdefault((-dx, -dy, -dz), []).append(lambda: pltpu.make_async_copy(zero, dst, s["rsem"].at[i]).start())
+            return Copy(src, dst, (gx + dx, gy + dy, gz + dz), has(dx, dy, dz))
+
+        class Stage:
+            def __init__(self, make, void, size):
+                self.copies = make()
+                self.i, self.void, self.size = stages[0], void, size
+                stages[0] += 1
+
+            def start(self):
+                for copy in self.copies:
+                    copy.start()
+
+            def drain(self):
+                for copy in self.copies:
+                    copy.sent()
 
             def arrive(self):
-                self.under(self.recv_if, lambda: self.make().wait_recv())
-
-            def sent(self):
-                self.under(self.send_if, lambda: self.make().wait_send())
-
-        def toward(dx, dy, dz, src, dst):
-            return Copy(src, dst, (gx + dx, gy + dy, gz + dz), has(dx, dy, dz), has(-dx, -dy, -dz))
-
-        def halo0(n, src):
+                all_of_it = self.void.at[0:self.size]
+                pltpu.make_async_copy(all_of_it, all_of_it, s["rsem"].at[self.i]).wait()
+
+        def halo0(n):
+            fields = 2 if n.start == 0 else 1
             copies = []
             for dx, dy in DIRS:
-                xs = slice(0, 8) if dx == 0 else (slice(4, 8) if dx > 0 else slice(0, 4))
-                ys = slice(0, 16) if dy == 0 else (slice(8, 16) if dy > 0 else slice(0, 8))
-                group = 0 if dy == 0 else (1 if dx == 0 else 2)
-                copies.append(toward(dx, dy, 0, src.at[xs, ys, :], s["nat0"].at[n, group, xs, ys, :]))
+                if dy == 0:
+                    xs = slice(4, 8) if dx > 0 else slice(0, 4)
+                    copies.append(toward(dx, dy, 0, s["cells"].at[n, xs], s["x0"].at[n, xs], s["zero16"].at[0:fields]))
+                    continue
+                face = 0 if dy > 0 else 4
+                if dx == 0:
+                    mine, to = slice(face, face + 4), slice(face, face + 4)
+                else:
+                    mine = slice(face + 2, face + 4) if dx > 0 else slice(face, face + 2)
+                    first = (8 if dx > 0 else 12) + (0 if dy > 0 else 2)
+                    to = slice(first, first + 2)
+                copies.append(toward(dx, dy, 0, s["pack0"].at[n, mine], s["y0"].at[n, to], s["zero8"].at[0:fields, 0:to.stop - to.start]))
             return copies
 
-        def slab_halo(n, slab, slabs):
-            return [toward(dx, dy, dz, slab.at[n, 0 if dz < 0 else 1], slabs.at[n, 1 if dz < 0 else 0, ALL.index((-dx, -dy))])
+        def slab_halo(slab, slabs, zero):
+            return [toward(dx, dy, dz, slab(0 if dz < 0 else 1, dy), slabs(1 if dz < 0 else 0, ALL.index((-dx, -dy))), zero)
                     for dx, dy in reversed(ALL) for dz in (-1, 1)]
 
         def plane1(n):
             copies = []
             for dx, dy in DIRS:
                 d = ALL.index((-dx, -dy))
-                copies.append(toward(dx, dy, 0, s["nat1"].at[n, 0:4], s["nat1"].at[n, 4 * d:4 * d + 4]))
+                copies.append(toward(dx, dy, 0, s["nat1"].at[n, 0:4], s["nat1"].at[n, 4 * d:4 * d + 4], s["zero8"].at[0]))
             return copies
 
         def far1(n):
@@ -270,44 +308,49 @@
             for dx, dy in FAR:
                 e = FAR.index((-dx, -dy))
                 i = 3 if dx > 0 else 0
-                copies.append(toward(dx, dy, 0, s["nat1"].at[n, i:i + 1], s["nat1"].at[n, 36 + e:37 + e]))
+                copies.append(toward(dx, dy, 0, s["nat1"].at[n, i:i + 1], s["nat1"].at[n, 36 + e:37 + e], s["zero8"].at[0, 0:1]))
             return copies
 
         def z_halo1():
-            return [toward(0, 0, -1, s["ext1"].at[8:16, :], s["ext1"].at[R1 - 8:R1, :]),
-                    toward(0, 0, 1, s["ext1"].at[R1 - 16:R1 - 8, :], s["ext1"].at[0:8, :])]
+            return [toward(0, 0, -1, s["ext1"].at[8:16, :], s["ext1"].at[R1 - 8:R1, :], s["zero_w"]),
+                    toward(0, 0, 1, s["ext1"].at[R1 - 16:R1 - 8, :], s["ext1"].at[0:8, :], s["zero_w"])]
 
         def yzline(n):
             mine = s["yz2"].at[n, 1, gy]
-            return [Copy(mine, s["yz2"].at[n, 1 - dz, gy], (gx, lax.rem(gy + d, ny), gz + dz), has(0, 0, dz), has(0, 0, -dz))
-                    for d in sorted(range(ny), key=lambda d: -min(d, ny - d)) for dz in (-1, 1, 0) if d or dz]
+            copies = []
+            for d in sorted(range(ny), key=lambda d: -min(d, ny - d)):
+                for dz in (-1, 1, 0):
+                    if d or dz:
+                        copies.append(Copy(mine, s["yz2"].at[n, 1 - dz, gy], (gx, lax.rem(gy + d, ny), gz + dz), has(0, 0, dz)))
+            i = stages[0]
+            for dz in (-1, 1):
+                for d in range(ny):
+                    absent.setdefault((0, 0, dz), []).append(
+                        lambda dz=dz, d=d: pltpu.make_async_copy(s["zero2"], s["yz2"].at[n, 1 + dz, d], s["rsem"].at[i]).start())
+            return copies
 
         def xline(n):
-            return [Copy(s["yz2"].at[n], s["xs2"].at[n, gx], (lax.rem(gx + d, nx), gy, gz), None, None)
+            return [Copy(s["yz2"].at[n], s["xs2"].at[n, gx], (lax.rem(gx + d, nx), gy, gz), None)
                     for d in sorted(range(1, nx), key=lambda d: -min(d, nx - d))]
 
-        def start(copies):
-            for copy in copies:
-                copy.start()
-
-        def arrive(copies):
-            done = [copy for copy in unsent if copy.started and copy not in copies]
-            for copy in done:
-                copy.sent()
-                unsent.remove(copy)
-            for copy in copies:
-                copy.arrive()
-
-        srcs = (rhs, coef, s["sol"])
-        srcs = (rhs, coef, s["sol"])
-        P0 = [halo0(n, srcs[n]) for n in range(3)]
-        S0 = [slab_halo(n, s["slab0"], s["slabs0"]) for n in range(3)]
-        P1 = [plane1(n) for n in range(3)]
-        S1 = [None] + [slab_halo(n, s["slab1"], s["slabs1"]) for n in (1, 2)]
-        F1 = far1(0)
-        Z1 = z_halo1()
-        Y2 = [yzline(n) for n in range(3)]
-        X2 = [xline(n) for n in range(3)]
+        E0, E1, Y2, X2 = {}, [], [], []
+        for first, fields in ((0, 2), (2, 1)):
+            n = slice(first, first + fields)
+            E0[first] = Stage(lambda: halo0(n) + slab_halo(lambda side, dy: s["slab0"].at[n, side, 1 if dy else 0],
+                                                           lambda side, d: s["slabs0"].at[n, side, d], s["zero8"].at[0:fields, 0]),
+                              s["void8"], 50 * fields)
+        for n in range(3):
+            if n:
+                E1.append(Stage(lambda: slab_halo(lambda side, dy: s["slab1"].at[n, side], lambda side, d: s["slabs1"].at[n, side, d],
+                                                  s["zero8"].at[0, 0]) + plane1(n), s["void8"], 50))
+            else:
+                E1.append(Stage(lambda: plane1(0) + far1(0), s["void8"], 38))
+            Y2.append(Stage(lambda: yzline(n), s["void2"], 3 * ny - 1))
+            X2.append(Stage(lambda: xline(n), s["void2"], (nx - 1) * 3 * ny))
+        Z1 = Stage(z_halo1, s["void8"], 4)
+
+        for k in ("zero16", "zero8", "zero2", "zero_w"):
+            s[k][...] = jnp.zeros(s[k].shape, F32)
 
         barrier = pltpu.get_barrier_semaphore()
         for d in range(1, nx):
@@ -332,73 +375,52 @@
             def _(dx=dx, dy=dy, dz=dz):
                 pl.semaphore_signal(barrier, inc=1, device_id=(gx + dx, gy + dy, gz + dz), device_id_type=MESH)
 
-        for k in ["coef", "rhs", "kx1", "kx2", "kz1", "kz2", "place0"]:
-            loads[k].start()
-        for k in names:
-            if k not in ("kx1", "kx2", "kz1", "kz2", "place0"):
-                loads[k].start()
-
-        def clear(dx, dy, dz, dsts):
-            @pl.when(jnp.logical_not(has(dx, dy, dz)))
-            def _():
-                for ref, index in dsts:
-                    ref[index] = jnp.zeros(ref.at[index].shape, F32)
-
-        for dx, dy in DIRS:
-            xs = slice(0, 8) if dx == 0 else (slice(4, 8) if dx < 0 else slice(0, 4))
-            ys = slice(0, 16) if dy == 0 else (slice(8, 16) if dy < 0 else slice(0, 8))
-            group = 0 if dy == 0 else (1 if dx == 0 else 2)
-            d = ALL.index((dx, dy))
-            dsts = []
-            for n in range(3):
-                dsts.append((s["nat0"], (n, group, xs, ys)))
-                dsts.append((s["nat1"], (n, slice(4 * d, 4 * d + 4))))
-                for side in range(2):
-                    dsts.append((s["slabs0"], (n, side, d)))
-                    if n:
-                        dsts.append((s["slabs1"], (n, side, d)))
-            clear(dx, dy, 0, dsts)
-        for e, (dx, dy) in enumerate(FAR):
-            clear(dx, dy, 0, [(s["nat1"], (0, slice(36 + e, 37 + e)))])
-        for dz in (-1, 1):
-            side = 0 if dz < 0 else 1
-            dsts = [(s["ext1"], (slice(0, 8) if dz < 0 else slice(R1 - 8, R1),))]
-            for n in range(3):
-                dsts.append((s["slabs0"], (n, side)))
-                if n:
-                    dsts.append((s["slabs1"], (n, side)))
-                dsts.append((s["yz2"], (n, 1 + dz)))
-            clear(0, 0, dz, dsts)
+        for k in ("coef", "rhs", "early", "late"):
+            for load in loads[k]:
+                load.start()
+
+        for place, fills in absent.items():
+            @pl.when(jnp.logical_not(has(*place)))
+            def _(fills=fills):
+                for fill in fills:
+                    fill()
+
         s["nat1"][0, 42:48] = jnp.zeros((6, 8, 128), F32)
         for n in (1, 2):
             s["nat1"][n, 36:48] = jnp.zeros((12, 8, 128), F32)
 
+        def post0(n, nat, flipped):
+            cells = nat.reshape(8, 16, 128)
+            high, low = cells[:, 12:16].reshape(32, 128), cells[:, 0:4].reshape(32, 128)
+            s["pack0"][n, 0:4] = high.reshape(4, 8, 128)
+            s["pack0"][n, 4:8] = low.reshape(4, 8, 128)
+            faces = jnp.concatenate([high, low, high[16:32], low[16:32], high[0:16], low[0:16]], axis=0).T
+            for kind, rows in enumerate((flipped, faces)):
+                s["slab0"][n, 0, kind] = rows[0:8]
+                s["slab0"][n, 1, kind] = rows[120:128]
+
+        lane = lax.broadcasted_iota(jnp.int32, (8, 128), 1)
+
+        def by_quarter(parts):
+            return jnp.where(lane < 32, parts[0], jnp.where(lane < 64, parts[1], jnp.where(lane < 96, parts[2], parts[3])))
+
         ready("coef")
         k_nat = coef[...].reshape(128, 128)
         k_flip = k_nat.T
-        s["slab0"][1, 0] = k_flip[0:8]
-        s["slab0"][1, 1] = k_flip[120:128]
+        post0(1, k_nat, k_flip)
         ready("rhs")
-        f_flip = rhs[...].reshape(128, 128).T
-        s["slab0"][0, 0] = f_flip[0:8]
-        s["slab0"][0, 1] = f_flip[120:128]
-        pl.semaphore_wait(barrier, total)
-        start(S0[1])
-        start(P0[1])
-        start(S0[0])
-        start(P0[0])
+        f_nat = rhs[...].reshape(128, 128)
+        f_flip = f_nat.T
+        post0(0, f_nat, f_flip)
         k1 = times(left(c["kx1"][...], k_nat), c["kz1"][...])
         s["nat1"][0, 0:4] = k1.reshape(4, 8, 128)
-        start(P1[0])
-        start(F1)
         k2_parts = times(left(c["kx2"][...], k_nat), c["kz2"][...])
-        lane = lax.broadcasted_iota(jnp.int32, (8, 128), 1)
-
-        def by_quarter(parts):
-            return jnp.where(lane < 32, parts[0], jnp.where(lane < 64, parts[1], jnp.where(lane < 96, parts[2], parts[3])))
-
         s["yz2"][0, 1, gy] = by_quarter([k2_parts[8 * q:8 * q + 8] for q in range(4)])[0:2]
-        start(Y2[0])
+
+        pl.semaphore_wait(barrier, total)
+        E0[0].start()
+        E1[0].start()
+        Y2[0].start()
 
         def shifts(v, xe):
             rows, lanes = v.shape
@@ -445,17 +467,16 @@
             return jnp.broadcast_to(plane, z.shape) & (z >= 0) & (z < sizes[2])
 
         def assemble0(n, flipped):
-            blocks = [flipped] + [s["nat0"][n, i].reshape(128, 128).T for i in range(3)]
-            right = lane < 64
-            above = lax.rem(lane, 16) < 8
+            blocks = [flipped, s["x0"][n].reshape(128, 128).T, s["y0"][n].reshape(128, 128).T]
             ends = []
             for side in range(2):
                 def at(dx, dy, side=side):
                     return s["slabs0"][n, side, ALL.index((dx, dy))]
 
+                diagonals = jnp.where(lane < 80, at(-1, -1), jnp.where(lane < 96, at(-1, 1), jnp.where(lane < 112, at(1, -1), at(1, 1))))
                 ends.append(jnp.concatenate([
-                    at(0, 0), jnp.where(right, at(1, 0), at(-1, 0)), jnp.where(above, at(0, 1), at(0, -1)),
-                    jnp.where(right, jnp.where(above, at(1, 1), at(1, -1)), jnp.where(above, at(-1, 1), at(-1, -1)))], axis=1))
+                    at(0, 0), jnp.where(lane < 64, at(1, 0), at(-1, 0)),
+                    jnp.where(lane < 32, at(0, -1), jnp.where(lane < 64, at(0, 1), diagonals))], axis=1))
             wide = jnp.concatenate([ends[0], jnp.concatenate(blocks, axis=1), ends[1]], axis=0)
             return times(wide, c["place0"][...])
 
@@ -471,13 +492,17 @@
             wide = jnp.concatenate([ends[0], natural1(n), ends[1]], axis=0)
             return times(wide, c["place1"][...])
 
+        def drain(*done):
+            for stage in done:
+                stage.drain()
+
         def gather2_x(n):
-            arrive(Y2[n])
-            start(X2[n])
+            Y2[n].arrive()
+            X2[n].start()
             s["xs2"][n, gx] = s["yz2"][n]
 
         def gather2(n):
-            arrive(X2[n])
+            X2[n].arrive()
             rows = []
             for dz in range(3):
                 flipped = s["xs2"][n, :, dz].reshape(nx * ny * 2, 128).T
@@ -493,22 +518,17 @@
         xb = c["coord"][6:7, 0:l3]
         for i in (jnp.maximum(gz - 1, 0), gz, jnp.minimum(gz + 1, nz - 1)):
             pick = lax.broadcasted_iota(jnp.int32, (2 * ny * nz, l3), 0) == c["coord"][9:10, 0:l3] + i
-            picked = jnp.dot(agg[...].astype(F32).astype(BF16), jnp.where(pick, 1.0, 0.0).astype(BF16), preferred_element_type=F32)
+            picked = jnp.dot(s["agg"][...].astype(F32).astype(BF16), jnp.where(pick, 1.0, 0.0).astype(BF16), preferred_element_type=F32)
             mine = jnp.zeros((1, l3), F32)
             for r in range(nx // 2):
                 mine = jnp.where(xb // 2 == r, picked[r:r + 1], mine)
             near_owner.append(jnp.broadcast_to(mine, (16, l3)))
         owner = jnp.concatenate(near_owner, axis=0)
 
-        arrive(P1[0] + F1)
-        s["ext1"][8:R1 - 8] = times(natural1(0), c["place1"][...])
-        start(Z1)
-
-        arrive(P0[1] + S0[1])
+        E0[0].arrive()
         k0 = assemble0(1, k_flip)
         x0, y0, z0 = coords(0, L0, R0, 8 * gx, 16 * gy, 128 * gz - 8)
         setup(k0, XE0, 1.0, inside_of(x0, y0, z0, (8 * nx, 16 * ny, 128 * nz)), None, None, s["m0"], s["c0"])
-        arrive(P0[0] + S0[0])
         f0 = assemble0(0, f_flip)
         s["rhs0"][...] = f0
         s["c0"][2] = s["c0"][0] * f0
@@ -547,21 +567,25 @@
             half = halved(r, 8, 64)
             ends = times(jnp.concatenate([half[0:8], half[56:64]], axis=0), c["sel0r"][...])
             s["slab1"][n] = ends.reshape(2, 8, 128)
-            start(S1[n])
             s["nat1"][n, 0:4, :, 0:64] = select_t(c["sel0"][...], half).reshape(4, 8, 64)
-            start(P1[n])
+            E1[n].start()
             if cycle == 0:
+                E1[0].arrive()
+                s["ext1"][8:R1 - 8] = times(natural1(0), c["place1"][...])
+                Z1.start()
                 gather2_x(0)
-                arrive(Z1)
+                Z1.arrive()
                 inside = inside_of(x1, y1, z1, (4 * nx, 8 * ny, 64 * nz))
                 setup(s["ext1"][...], XE1, 0.25, inside, None, None, s["m1"], s["c1"])
-            arrive(P1[n] + S1[n])
+            if cycle == 1:
+                drain(X2[1])
+            E1[n].arrive()
             s["c1"][2] = s["c1"][0] * assemble1(n)
             v = down(s["m1"], s["c1"], XE1)
             half = halved(residual(v, s["c1"][2], s["m1"], s["c1"], XE1), 8, 32)
             quarters = [jnp.where(c["coord"][10 + q:11 + q, 0:L1] > 0, half, 0.0) for q in range(4)]
             s["yz2"][n, 1, gy] = select_t(c["sel1"][...], jnp.concatenate(quarters, axis=0))[0:2]
-            start(Y2[n])
+            Y2[n].start()
             if cycle == 0:
                 k2 = gather2(0)
                 x, y, z = coords(2, l2, R2, 0, 0, 32 * gz - 32)
@@ -572,7 +596,15 @@
                 inner = [jnp.broadcast_to(q, z.shape) for q in (x + 1 < nx, x > 0, y + 1 < 2 * ny, y > 0)]
                 same = [other == owner for other in shifts(owner, nx)]
                 setup(k3, nx, 0.015625, inside_of(x, y, z, (nx, 2 * ny, 16 * nz)), inner, same, s["m3"], s["c3"])
+            if cycle == 0:
+                drain(E0[0], E1[0], Y2[0], Z1)
+            else:
+                drain(E0[2])
             gather2_x(n)
+            if cycle == 0:
+                drain(E1[1], X2[0])
+            else:
+                drain(E1[2], Y2[2])
             f2 = gather2(n)
             s["c2"][2] = s["c2"][0] * f2
             v2 = down(s["m2"], s["c2"], x2)
@@ -595,21 +627,19 @@
                 v = sweep(v, s["c0"][2], s["m0"], XE0)
             nat = select_t(c["unsel"][...], v[8:R0 - 8])
             if cycle == 0:
-                s["sol"][...] = nat.reshape(8, 16, 128)
+                s["cells"][2] = nat.reshape(8, 16, 128)
                 flipped = nat.T
-                s["slab0"][2, 0] = flipped[0:8]
-                s["slab0"][2, 1] = flipped[120:128]
-                start(S0[2])
-                start(P0[2])
-                arrive(P0[2] + S0[2])
+                post0(2, nat, flipped)
+                E0[2].start()
+                drain(Y2[1])
+                E0[2].arrive()
                 now = assemble0(2, flipped)
                 s["c0"][2] = sweep(now, s["c0"][0] * s["rhs0"][...], s["m0"], XE0) - now
             else:
-                out[...] = s["sol"][...] + nat.reshape(8, 16, 128)
+                out[...] = s["cells"][2] + nat.reshape(8, 16, 128)
         for k in loads:
             ready(k)
-        for copy in unsent:
-            copy.sent()
+        X2[2].drain()
 
     vmem = pl.BlockSpec(memory_space=pltpu.VMEM)
     hbm = pl.BlockSpec(memory_space=pl.ANY)
@@ -619,7 +649,7 @@
         return pl.pallas_call(
             kernel,
             out_shape=pltpu.VMEM((8, 16, 128), F32),
-            in_specs=[hbm, hbm, vmem] + [hbm] * len(names),
+            in_specs=[hbm, hbm, hbm] + [hbm] * len(names),
             out_specs=vmem,
             scratch_shapes=[scratch[k] for k in keys] + held,
             compiler_params=pltpu.CompilerParams(collective_id=0, has_side_effects=True, vmem_limit_bytes=60 * 1024 * 1024),

time: 73.1 us -> 63.1 us (0.86)
  Pallas kernels: 72.3 us -> 62.4 us
    pallas_call x1, Pallas kernels: 72.3 us -> 62.4 us  [body(): pl.pallas_call(kernel, out_shape=pltpu.VMEM((8, 16, 128), F32), in_specs=...]
where the time goes in v3:
time: 63.1 us; the launch traced here: 63 us
  Pallas kernels  62.4 us (99%)
    pallas_call x1, Pallas kernels, body(): pl.pallas_call(kernel, out_shape=pltpu.VMEM((8, 16, 128), F32), in_specs=...  62.4 us

profile of v3, /device:TPU:1, one launch (start us, length us, event | category | flops | bytes accessed | tf_op | source)
XLA Modules:
  0.0 63.0 jit_solution(13356160034911158194)
XLA Ops:
  0.0 62.4 %shard_map.172 = f32[8,16,128]{2,1,0:T(8,128)S(1)} custom-call(f32[8,16,128]{2,1,0:T(8,128)} %rhs_hbm.1, f32[8,16,128]{2,1,0:T(8,128)} %coef_hbm.1, s32[4,128]{1,0:T(4,128)} %bitcast.1, bf16[384,128]{1,0:T(8,128)(2,1)} %constant.30.clone.rest_0_, bf16[384,384]{1,0:T(8,128)(2,1)} %constant.31.clone.rest_1_, bf16[32,384]{1,0:T(8,128)(2,1)} %constant.32.clone.rest_2_, ...), custom_call_target="tpu_custom_call" | custom-call | tf_op jit(solution)/shard_map/pallas_call | solution.py:649
  62.4 0.6 %copy.20 = f32[8,16,128]{2,1,0:T(8,128)} copy(f32[8,16,128]{2,1,0:T(8,128)S(1)} %shard_map.172) | data formatting | bytes 131072

commit v4 on v3

--- a/solution.py
+++ b/solution.py
@@ -13,6 +13,8 @@
 COARSE_SWEEPS = 8
 DIRS = [(dx, dy) for dx in (-1, 0, 1) for dy in (-1, 0, 1) if (dx, dy) != (0, 0)]
 ALL = [(0, 0)] + DIRS
+CORNERS = [d for d in DIRS if d[0] and d[1]]
+BESIDE = [d for d in ALL if d not in CORNERS]
 FAR = [(dx, dy) for dx in (-2, 2) for dy in (-1, 0, 1)]
 XE0, YE0, H0 = 16, 24, 4
 XE1, YE1, H1 = 14, 18, 5
@@ -117,6 +119,8 @@
             coord[6:8, y * nx + x] = x, y
             coord[9, y * nx + x] = (x % 2) * ny * nz + (y // 2) * nz
     coord[10:14, 0:L1] = quarter[0:4]
+    k = np.arange(nx * ny * 8)
+    coord[14, 0:len(k)] = k // 2 % ny
     sel0r = np.concatenate([sel0] * 4, axis=0).T
     names = dict(sel0r=sel0r, place0=place0, sel0=sel0, unsel=unsel, place1=place1, sel1=sel1, prol0=prol0, perm2=perm2, rest2=rest2,
                  prol2=prol2, kx1=kx1, kx2=kx2.reshape(32, 128), kz1=kz1, kz2=kz2)
@@ -153,7 +157,7 @@
     consts = tables(nx, ny, nz)
     names = list(consts)
 
-    n_sem = 13
+    n_sem = 19
 
     scratch = dict(
         x0=pltpu.VMEM((3, 8, 16, 128), F32),
@@ -166,15 +170,18 @@
         slab1=pltpu.VMEM((3, 2, 8, 128), F32),
         slabs1=pltpu.VMEM((3, 2, 9, 8, 128), F32),
         ext1=pltpu.VMEM((R1, L1), F32),
-        yz2=pltpu.VMEM((3, 3, ny, 2, 128), F32),
-        xs2=pltpu.VMEM((3, nx, 3, ny, 2, 128), F32),
+        yz2=pltpu.VMEM((3, 3, ny + 8, 2, 128), F32),
+        xs2=pltpu.VMEM((3, nx, 3, ny + 8, 2, 128), F32),
         cells=pltpu.VMEM((3, 8, 16, 128), F32),
         m0=pltpu.VMEM((6, R0, L0), F32),
-        c0=pltpu.VMEM((4, R0, L0), F32),
+        c0=pltpu.VMEM((3, R0, L0), F32),
         m1=pltpu.VMEM((6, R1, L1), F32),
-        c1=pltpu.VMEM((4, R1, L1), F32),
+        c1=pltpu.VMEM((3, R1, L1), F32),
         m2=pltpu.VMEM((6, R2, l2), F32),
-        c2=pltpu.VMEM((4, R2, l2), F32),
+        c2=pltpu.VMEM((3, R2, l2), F32),
+        v0=pltpu.VMEM((2, L0 // 128, R0 + 16, 128), F32),
+        v1=pltpu.VMEM((2, L1 // 128, R1 + 16, 128), F32),
+        v2=pltpu.VMEM((2, l2 // 128, R2 + 16, 128), F32),
         m3=pltpu.VMEM((6, R3, l3), F32),
         c3=pltpu.VMEM((2, R3, l3), F32),
         pairs=pltpu.VMEM((max(L0, l2) // 128, 160, 128), F32),
@@ -185,7 +192,7 @@
         zero2=pltpu.VMEM((2, 128), F32),
         zero_w=pltpu.VMEM((8, L1), F32),
         void8=pltpu.VMEM((104, 8, 128), F32),
-        void2=pltpu.VMEM((max(nx, 2) * 3 * ny, 2, 128), F32),
+        void2=pltpu.VMEM((max(nx * 3 * ny, nx * 15, 16), 2, 128), F32),
         lsem=pltpu.SemaphoreType.DMA((4,)),
         ssem=pltpu.SemaphoreType.DMA((n_sem,)),
         rsem=pltpu.SemaphoreType.DMA((n_sem,)),
@@ -228,6 +235,8 @@
                     ok = here if ok is None else ok & here
             return ok
 
+        for k in ("coef", "rhs"):
+            loads[k][0].start()
         stages = [0]
         absent = {}
 
@@ -238,6 +247,7 @@
                     src_ref=src, dst_ref=dst, send_sem=s["ssem"].at[i], recv_sem=s["rsem"].at[i],
                     device_id=there, device_id_type=MESH)
                 self.send_if = send_if
+                self.hops = 0
 
             def under(self, f):
                 if self.send_if is None:
@@ -254,11 +264,13 @@
         def toward(dx, dy, dz, src, dst, zero):
             i = stages[0]
             absent.setdefault((-dx, -dy, -dz), []).append(lambda: pltpu.make_async_copy(zero, dst, s["rsem"].at[i]).start())
-            return Copy(src, dst, (gx + dx, gy + dy, gz + dz), has(dx, dy, dz))
+            copy = Copy(src, dst, (gx + dx, gy + dy, gz + dz), has(dx, dy, dz))
+            copy.hops = abs(dx) + abs(dy) + abs(dz)
+            return copy
 
         class Stage:
             def __init__(self, make, void, size):
-                self.copies = make()
+                self.copies = sorted(make(), key=lambda copy: -copy.hops)
                 self.i, self.void, self.size = stages[0], void, size
                 stages[0] += 1
 
@@ -292,9 +304,9 @@
                 copies.append(toward(dx, dy, 0, s["pack0"].at[n, mine], s["y0"].at[n, to], s["zero8"].at[0:fields, 0:to.stop - to.start]))
             return copies
 
-        def slab_halo(slab, slabs, zero):
+        def slab_halo(slab, slabs, zero, planes=ALL):
             return [toward(dx, dy, dz, slab(0 if dz < 0 else 1, dy), slabs(1 if dz < 0 else 0, ALL.index((-dx, -dy))), zero)
-                    for dx, dy in reversed(ALL) for dz in (-1, 1)]
+                    for dx, dy in planes for dz in (-1, 1)]
 
         def plane1(n):
             copies = []
@@ -315,25 +327,42 @@
             return [toward(0, 0, -1, s["ext1"].at[8:16, :], s["ext1"].at[R1 - 8:R1, :], s["zero_w"]),
                     toward(0, 0, 1, s["ext1"].at[R1 - 16:R1 - 8, :], s["ext1"].at[0:8, :], s["zero_w"])]
 
-        def yzline(n):
-            mine = s["yz2"].at[n, 1, gy]
+        def yzline():
+            mine = s["yz2"].at[0, 1, gy + 4]
             copies = []
             for d in sorted(range(ny), key=lambda d: -min(d, ny - d)):
                 for dz in (-1, 1, 0):
                     if d or dz:
-                        copies.append(Copy(mine, s["yz2"].at[n, 1 - dz, gy], (gx, lax.rem(gy + d, ny), gz + dz), has(0, 0, dz)))
+                        copies.append(Copy(mine, s["yz2"].at[0, 1 - dz, gy + 4], (gx, lax.rem(gy + d, ny), gz + dz), has(0, 0, dz)))
             i = stages[0]
             for dz in (-1, 1):
                 for d in range(ny):
                     absent.setdefault((0, 0, dz), []).append(
-                        lambda dz=dz, d=d: pltpu.make_async_copy(s["zero2"], s["yz2"].at[n, 1 + dz, d], s["rsem"].at[i]).start())
+                        lambda dz=dz, d=d: pltpu.make_async_copy(s["zero2"], s["yz2"].at[0, 1 + dz, 4 + d], s["rsem"].at[i]).start())
             return copies
 
-        def xline(n):
-            return [Copy(s["yz2"].at[n], s["xs2"].at[n, gx], (lax.rem(gx + d, nx), gy, gz), None)
-                    for d in sorted(range(1, nx), key=lambda d: -min(d, nx - d))]
-
-        E0, E1, Y2, X2 = {}, [], [], []
+        def yzwindow(n, offsets):
+            copies = []
+            i = stages[0]
+            for dy in offsets:
+                for dz in (-1, 1, 0):
+                    if dy or dz:
+                        copy = Copy(s["yz2"].at[n, 1, gy + 4], s["yz2"].at[n, 1 - dz, gy + 4], (gx, gy + dy, gz + dz), has(0, dy, dz))
+                        copy.hops = abs(dy) + abs(dz)
+                        copies.append(copy)
+                        absent.setdefault((0, dy, dz), []).append(
+                            lambda dy=dy, dz=dz: pltpu.make_async_copy(s["zero2"], s["yz2"].at[n, 1 + dz, gy + dy + 4], s["rsem"].at[i]).start())
+            return copies
+
+        def xline(n, windows):
+            copies = []
+            for d in sorted(range(1, nx), key=lambda d: -min(d, nx - d)):
+                for first, size in windows:
+                    at = pl.ds(first, size)
+                    copies.append(Copy(s["yz2"].at[n, :, at], s["xs2"].at[n, gx, :, at], (lax.rem(gx + d, nx), gy, gz), None))
+            return copies
+
+        E0, E1, C1, Y2, X2, YF, XF = {}, [], [None], [], [], [None], [None]
         for first, fields in ((0, 2), (2, 1)):
             n = slice(first, first + fields)
             E0[first] = Stage(lambda: halo0(n) + slab_halo(lambda side, dy: s["slab0"].at[n, side, 1 if dy else 0],
@@ -341,31 +370,39 @@
                               s["void8"], 50 * fields)
         for n in range(3):
             if n:
-                E1.append(Stage(lambda: slab_halo(lambda side, dy: s["slab1"].at[n, side], lambda side, d: s["slabs1"].at[n, side, d],
-                                                  s["zero8"].at[0, 0]) + plane1(n), s["void8"], 50))
+                ends = (lambda side, dy: s["slab1"].at[n, side], lambda side, d: s["slabs1"].at[n, side, d], s["zero8"].at[0, 0])
+                E1.append(Stage(lambda: slab_halo(*ends, BESIDE) + plane1(n), s["void8"], 42))
+                C1.append(Stage(lambda: slab_halo(*ends, CORNERS), s["void8"], 8))
             else:
                 E1.append(Stage(lambda: plane1(0) + far1(0), s["void8"], 38))
-            Y2.append(Stage(lambda: yzline(n), s["void2"], 3 * ny - 1))
-            X2.append(Stage(lambda: xline(n), s["void2"], (nx - 1) * 3 * ny))
+            if n:
+                YF.append(Stage(lambda: yzwindow(n, (-4, -3, 3, 4)), s["void2"], 12))
+                Y2.append(Stage(lambda: yzwindow(n, (-2, -1, 0, 1, 2)), s["void2"], 14))
+                X2.append(Stage(lambda: xline(n, [(gy + 2, 5)]), s["void2"], (nx - 1) * 15))
+                XF.append(Stage(lambda: xline(n, [(gy, 2), (gy + 7, 2)]), s["void2"], (nx - 1) * 12))
+            else:
+                Y2.append(Stage(yzline, s["void2"], 3 * ny - 1))
+                X2.append(Stage(lambda: xline(0, [(4, ny)]), s["void2"], (nx - 1) * 3 * ny))
         Z1 = Stage(z_halo1, s["void8"], 4)
 
         for k in ("zero16", "zero8", "zero2", "zero_w"):
             s[k][...] = jnp.zeros(s[k].shape, F32)
 
         barrier = pltpu.get_barrier_semaphore()
-        for d in range(1, nx):
-            pl.semaphore_signal(barrier, inc=1, device_id=(lax.rem(gx + d, nx), gy, gz), device_id_type=MESH)
-        for d in range(1, ny):
-            pl.semaphore_signal(barrier, inc=1, device_id=(gx, lax.rem(gy + d, ny), gz), device_id_type=MESH)
         total = jnp.int32(nx - 1 + ny - 1)
+        by_distance = sorted(range(ny), key=lambda d: -min(d, ny - d))
         for dz in (-1, 1):
             ok = has(0, 0, dz)
             total = total + ny * ok.astype(jnp.int32)
 
             @pl.when(ok)
             def _(dz=dz):
-                for d in range(ny):
+                for d in by_distance:
                     pl.semaphore_signal(barrier, inc=1, device_id=(gx, lax.rem(gy + d, ny), gz + dz), device_id_type=MESH)
+        for d in by_distance[:-1]:
+            pl.semaphore_signal(barrier, inc=1, device_id=(gx, lax.rem(gy + d, ny), gz), device_id_type=MESH)
+        for d in range(1, nx):
+            pl.semaphore_signal(barrier, inc=1, device_id=(lax.rem(gx + d, nx), gy, gz), device_id_type=MESH)
         near = [(dx, dy, 0) for dx, dy in DIRS + FAR if dx and dy] + [(dx, dy, dz) for dx, dy in DIRS if dx for dz in (-1, 1)]
         for dx, dy, dz in near:
             ok = has(dx, dy, dz)
@@ -375,16 +412,16 @@
             def _(dx=dx, dy=dy, dz=dz):
                 pl.semaphore_signal(barrier, inc=1, device_id=(gx + dx, gy + dy, gz + dz), device_id_type=MESH)
 
-        for k in ("coef", "rhs", "early", "late"):
+        for k in ("early", "late"):
             for load in loads[k]:
                 load.start()
 
-        for place, fills in absent.items():
-            @pl.when(jnp.logical_not(has(*place)))
-            def _(fills=fills):
-                for fill in fills:
-                    fill()
-
+        for k in ("v0", "v1", "v2"):
+            rows = s[k].shape[2]
+            for b in range(2):
+                for j in range(s[k].shape[1]):
+                    s[k][b, j, 0:8] = jnp.zeros((8, 128), F32)
+                    s[k][b, j, rows - 8:rows] = jnp.zeros((8, 128), F32)
         s["nat1"][0, 42:48] = jnp.zeros((6, 8, 128), F32)
         for n in (1, 2):
             s["nat1"][n, 36:48] = jnp.zeros((12, 8, 128), F32)
@@ -412,19 +449,29 @@
         f_nat = rhs[...].reshape(128, 128)
         f_flip = f_nat.T
         post0(0, f_nat, f_flip)
+        pl.semaphore_wait(barrier, total)
+        E0[0].start()
+        for place, fills in absent.items():
+            @pl.when(jnp.logical_not(has(*place)))
+            def _(fills=fills):
+                for fill in fills:
+                    fill()
+
         k1 = times(left(c["kx1"][...], k_nat), c["kz1"][...])
         s["nat1"][0, 0:4] = k1.reshape(4, 8, 128)
+        E1[0].start()
         k2_parts = times(left(c["kx2"][...], k_nat), c["kz2"][...])
-        s["yz2"][0, 1, gy] = by_quarter([k2_parts[8 * q:8 * q + 8] for q in range(4)])[0:2]
-
-        pl.semaphore_wait(barrier, total)
-        E0[0].start()
-        E1[0].start()
+        s["yz2"][0, 1, gy + 4] = by_quarter([k2_parts[8 * q:8 * q + 8] for q in range(4)])[0:2]
         Y2[0].start()
 
         def shifts(v, xe):
             rows, lanes = v.shape
-            return (pltpu.roll(v, lanes - 1, 1), pltpu.roll(v, 1, 1), pltpu.roll(v, lanes - xe, 1), pltpu.roll(v, xe, 1),
+            tiles = [v[:, i:i + 128] for i in range(0, lanes, 128)]
+            if 128 % xe or len(tiles) == 1:
+                beside = (pltpu.roll(v, lanes - 1, 1), pltpu.roll(v, 1, 1))
+            else:
+                beside = tuple(jnp.concatenate([pltpu.roll(tile, d, 1) for tile in tiles], axis=1) for d in (127, 1))
+            return beside + (pltpu.roll(v, lanes - xe, 1), pltpu.roll(v, xe, 1),
                     pltpu.roll(v, rows - 1, 0), pltpu.roll(v, 1, 0))
 
         def setup(k, xe, factor, inside, inner, extra, m, consts_ref):
@@ -450,11 +497,46 @@
             if consts_ref.shape[0] > 2:
                 consts_ref[1] = 1.25 * diag
 
-        def sweep(v, g, m, xe):
+        def sweep(v, g, m, xe, first=0):
             total = 0.2 * v + g
             for i, other in enumerate(shifts(v, xe)):
-                total = total + m[i] * other
+                total = total + m[i, first:first + v.shape[0]] * other
             return total
+
+        def put(vs, k, value, first=0):
+            for j in range(vs.shape[1]):
+                vs[k, j, 8 + first:8 + first + value.shape[0]] = value[:, 128 * j:128 * j + 128]
+
+        def get(vs, k, rows, first=0):
+            parts = [vs[k, j, 8 + first:8 + first + rows] for j in range(vs.shape[1])]
+            return parts[0] if len(parts) == 1 else jnp.concatenate(parts, axis=1)
+
+        def sweep_in(vs, a, b, g, m, xe, rows, first=0):
+            count = vs.shape[1]
+
+            def body(i, carry):
+                row = first + 8 * i
+                at = pl.ds(pl.multiple_of(row, 8), 8)
+                centre = [vs[a, j, pl.ds(row + 8, 8), :] for j in range(count)]
+                right, left_, above, below = ([pltpu.roll(v, d, 1) for v in centre] for d in (127, 1, 128 - xe, xe))
+                for j in range(count):
+                    after, before = (j + 1) % count, (j - 1) % count
+                    lanes = slice(128 * j, 128 * j + 128)
+                    xr, xl, yr, yl = right[j], left_[j], above[j], below[j]
+                    if count > 1:
+                        if 128 % xe:
+                            xr = jnp.where(lane < 127, xr, right[after])
+                            xl = jnp.where(lane > 0, xl, left_[before])
+                        yr = jnp.where(lane < 128 - xe, yr, above[after])
+                        yl = jnp.where(lane >= xe, yl, below[before])
+                    total = 0.2 * centre[j] + g[at, lanes]
+                    others = (xr, xl, yr, yl, vs[a, j, pl.ds(row + 9, 8), :], vs[a, j, pl.ds(row + 7, 8), :])
+                    for q, other in enumerate(others):
+                        total = total + m[q, at, lanes] * other
+                    vs[b, j, pl.ds(row + 8, 8), :] = total
+                return carry
+
+            lax.fori_loop(0, rows // 8, body, 0, unroll=True)
 
         def coords(level, lanes, rows, x_off, y_off, z_off):
             x = c["coord"][2 * level:2 * level + 1, 0:lanes] + x_off
@@ -484,13 +566,21 @@
             nat = s["nat1"][n].reshape(384, 128)
             return jnp.concatenate([nat[128 * i:128 * i + 128].T for i in range(3)], axis=1)[0:64]
 
+        def slabs_of(n, side, planes):
+            slabs = [s["slabs1"][n, side, d] if ALL[d] in planes else jnp.zeros((8, 128), F32) for d in range(9)]
+            return jnp.concatenate([by_quarter(slabs[0:4]), by_quarter(slabs[4:8]), jnp.where(lane < 32, slabs[8], 0.0)], axis=1)
+
         def assemble1(n):
-            ends = []
-            for side in range(2):
-                slabs = [s["slabs1"][n, side, d] for d in range(9)]
-                ends.append(jnp.concatenate([by_quarter(slabs[0:4]), by_quarter(slabs[4:8]), jnp.where(lane < 32, slabs[8], 0.0)], axis=1))
+            ends = [slabs_of(n, side, BESIDE) for side in range(2)]
             wide = jnp.concatenate([ends[0], natural1(n), ends[1]], axis=0)
             return times(wide, c["place1"][...])
+
+        def corners1(n):
+            C1[n].arrive()
+            more = times(jnp.concatenate([slabs_of(n, side, CORNERS) for side in range(2)], axis=0), c["place1"][...])
+            for rows, part in ((slice(0, 8), more[0:8]), (slice(R1 - 8, R1), more[8:16])):
+                s["c1"][2, rows] = s["c1"][2, rows] + s["c1"][0, rows] * part
+            presmooth(s["v1"], s["m1"], s["c1"], XE1)
 
         def drain(*done):
             for stage in done:
@@ -499,15 +589,24 @@
         def gather2_x(n):
             Y2[n].arrive()
             X2[n].start()
+            if n:
+                YF[n].arrive()
+                XF[n].start()
             s["xs2"][n, gx] = s["yz2"][n]
 
         def gather2(n):
             X2[n].arrive()
+            if n:
+                XF[n].arrive()
             rows = []
             for dz in range(3):
-                flipped = s["xs2"][n, :, dz].reshape(nx * ny * 2, 128).T
+                flipped = s["xs2"][n, :, dz, 4:4 + ny].reshape(nx * ny * 2, 128).T
                 rows.append(jnp.concatenate([flipped[32 * q:32 * q + 32] for q in range(4)], axis=1))
-            return times(jnp.concatenate(rows, axis=0), c["perm2"][...])
+            wide = jnp.concatenate(rows, axis=0)
+            if n:
+                device = c["coord"][14:15, 0:wide.shape[1]] - gy
+                wide = jnp.where((device >= -4) & (device <= 4), wide, 0.0)
+            return times(wide, c["perm2"][...])
 
         x1, y1, z1 = coords(1, L1, R1, 4 * gx, 8 * gy, 64 * gz - 8)
         target = c["coord"][8:9, 0:L1] + (2 * gx + 4 * gy * x2)
@@ -551,40 +650,49 @@
                 parts.append(s["pairs"][j, first:first + rows])
             return parts[0] if len(parts) == 1 else jnp.concatenate(parts, axis=1)
 
-        def down(m, consts_ref, xe):
-            g = consts_ref[2]
-            v = sweep(g, g, m, xe)
-            consts_ref[3] = v
-            return v
-
-        def residual(v, g, m, consts_ref, xe):
-            return consts_ref[1] * (sweep(v, g, m, xe) - v)
+        def presmooth(vs, m, consts_ref, xe):
+            put(vs, 0, consts_ref[2])
+            sweep_in(vs, 0, 1, consts_ref.at[2], m, xe, m.shape[1])
+
+        def down(vs, m, consts_ref, xe):
+            rows = m.shape[1]
+            presmooth(vs, m, consts_ref, xe)
+            sweep_in(vs, 1, 0, consts_ref.at[2], m, xe, rows)
+            return consts_ref[1] * (get(vs, 0, rows) - get(vs, 1, rows))
+
+        def up(vs, m, consts_ref, xe, correction, first=0):
+            rows = correction.shape[0]
+            put(vs, 0, get(vs, 1, rows, first) + correction, first)
+            sweep_in(vs, 0, 1, consts_ref.at[2], m, xe, rows, first)
+            sweep_in(vs, 1, 0, consts_ref.at[2], m, xe, rows, first)
+            return get(vs, 0, rows, first)
+
+        E1[0].arrive()
+        s["ext1"][8:R1 - 8] = times(natural1(0), c["place1"][...])
+        Z1.start()
 
         for cycle in range(2):
             n = 1 + cycle
-            v = down(s["m0"], s["c0"], XE0)
-            r = residual(v, s["c0"][2], s["m0"], s["c0"], XE0)
+            r = down(s["v0"], s["m0"], s["c0"], XE0)
             half = halved(r, 8, 64)
             ends = times(jnp.concatenate([half[0:8], half[56:64]], axis=0), c["sel0r"][...])
             s["slab1"][n] = ends.reshape(2, 8, 128)
             s["nat1"][n, 0:4, :, 0:64] = select_t(c["sel0"][...], half).reshape(4, 8, 64)
             E1[n].start()
+            C1[n].start()
             if cycle == 0:
-                E1[0].arrive()
-                s["ext1"][8:R1 - 8] = times(natural1(0), c["place1"][...])
-                Z1.start()
                 gather2_x(0)
                 Z1.arrive()
                 inside = inside_of(x1, y1, z1, (4 * nx, 8 * ny, 64 * nz))
                 setup(s["ext1"][...], XE1, 0.25, inside, None, None, s["m1"], s["c1"])
             if cycle == 1:
-                drain(X2[1])
+                drain(X2[1], XF[1])
             E1[n].arrive()
             s["c1"][2] = s["c1"][0] * assemble1(n)
-            v = down(s["m1"], s["c1"], XE1)
-            half = halved(residual(v, s["c1"][2], s["m1"], s["c1"], XE1), 8, 32)
+            half = halved(down(s["v1"], s["m1"], s["c1"], XE1), 8, 32)
             quarters = [jnp.where(c["coord"][10 + q:11 + q, 0:L1] > 0, half, 0.0) for q in range(4)]
-            s["yz2"][n, 1, gy] = select_t(c["sel1"][...], jnp.concatenate(quarters, axis=0))[0:2]
+            s["yz2"][n, 1, gy + 4] = select_t(c["sel1"][...], jnp.concatenate(quarters, axis=0))[0:2]
+            YF[n].start()
             Y2[n].start()
             if cycle == 0:
                 k2 = gather2(0)
@@ -600,46 +708,42 @@
                 drain(E0[0], E1[0], Y2[0], Z1)
             else:
                 drain(E0[2])
+            corners1(n)
             gather2_x(n)
             if cycle == 0:
-                drain(E1[1], X2[0])
+                drain(E1[1], C1[1], X2[0])
             else:
-                drain(E1[2], Y2[2])
+                drain(E1[2], C1[2], Y2[2], YF[2])
             f2 = gather2(n)
             s["c2"][2] = s["c2"][0] * f2
-            v2 = down(s["m2"], s["c2"], x2)
-            r = residual(v2, s["c2"][2], s["m2"], s["c2"], x2)
+            r = down(s["v2"], s["m2"], s["c2"], x2)
             g3 = s["c3"][0] * times(halved(r, 0, R3), c["rest2"][...])
             e = g3
             for j in range(COARSE_SWEEPS - 1):
                 e = sweep(e, g3, s["m3"], nx)
-            fine = times(e, c["prol2"][...])
-            v = s["c2"][3] + doubled(fine, 0, R2)
-            for j in range(2):
-                v = sweep(v, s["c2"][2], s["m2"], x2)
-            fine = times(v[24:72], s["prol1"][...])
-            v = s["c1"][3] + doubled(fine, 8, R1)
-            for j in range(2):
-                v = sweep(v, s["c1"][2], s["m1"], XE1)
+            v = up(s["v2"], s["m2"], s["c2"], x2, doubled(times(e[8:40], c["prol2"][...]), 8, 48), 24)
+            fine = times(v, s["prol1"][...])
+            v = up(s["v1"], s["m1"], s["c1"], XE1, doubled(fine, 8, R1))
             fine = times(v, c["prol0"][...])
-            v = s["c0"][3] + doubled(fine, 8, R0)
-            for j in range(2):
-                v = sweep(v, s["c0"][2], s["m0"], XE0)
+            v = up(s["v0"], s["m0"], s["c0"], XE0, doubled(fine, 8, R0))
             nat = select_t(c["unsel"][...], v[8:R0 - 8])
             if cycle == 0:
                 s["cells"][2] = nat.reshape(8, 16, 128)
                 flipped = nat.T
                 post0(2, nat, flipped)
                 E0[2].start()
-                drain(Y2[1])
+                drain(Y2[1], YF[1])
                 E0[2].arrive()
                 now = assemble0(2, flipped)
-                s["c0"][2] = sweep(now, s["c0"][0] * s["rhs0"][...], s["m0"], XE0) - now
+                put(s["v0"], 0, now)
+                s["c0"][2] = s["c0"][0] * s["rhs0"][...]
+                sweep_in(s["v0"], 0, 1, s["c0"].at[2], s["m0"], XE0, R0)
+                s["c0"][2] = get(s["v0"], 1, R0) - get(s["v0"], 0, R0)
             else:
                 out[...] = s["cells"][2] + nat.reshape(8, 16, 128)
         for k in loads:
             ready(k)
-        X2[2].drain()
+        drain(X2[2], XF[2])
 
     vmem = pl.BlockSpec(memory_space=pltpu.VMEM)
     hbm = pl.BlockSpec(memory_space=pl.ANY)

time: 63.1 us -> 62.8 us (level)
  no operation moved by 1% of the time
where the time goes in v4:
time: 62.8 us; the launch traced here: 62.6 us
  Pallas kernels  62 us (99%)
  local copies, waits for them, and re-layouts  0.63 us (1%)
    pallas_call x1, Pallas kernels, body(): pl.pallas_call(kernel, out_shape=pltpu.VMEM((8, 16, 128), F32), in_specs=...  62 us

profile of v4, /device:TPU:1, one launch (start us, length us, event | category | flops | bytes accessed | tf_op | source)
XLA Modules:
  0.0 62.6 jit_solution(8550285754045337770)
XLA Ops:
  0.0 62.0 %shard_map.172 = f32[8,16,128]{2,1,0:T(8,128)S(1)} custom-call(f32[8,16,128]{2,1,0:T(8,128)} %rhs_hbm.1, f32[8,16,128]{2,1,0:T(8,128)} %coef_hbm.1, s32[4,128]{1,0:T(4,128)} %bitcast.1, bf16[384,128]{1,0:T(8,128)(2,1)} %constant.30.clone.rest_0_, bf16[384,384]{1,0:T(8,128)(2,1)} %constant.31.clone.rest_1_, bf16[32,384]{1,0:T(8,128)(2,1)} %constant.32.clone.rest_2_, ...), custom_call_target="tpu_custom_call" | custom-call | tf_op jit(solution)/shard_map/pallas_call | solution.py:753
  62.0 0.6 %copy.20 = f32[8,16,128]{2,1,0:T(8,128)} copy(f32[8,16,128]{2,1,0:T(8,128)S(1)} %shard_map.172) | data formatting | bytes 131072

commit v5 on v4

--- a/solution.py
+++ b/solution.py
@@ -184,7 +184,7 @@
         v2=pltpu.VMEM((2, l2 // 128, R2 + 16, 128), F32),
         m3=pltpu.VMEM((6, R3, l3), F32),
         c3=pltpu.VMEM((2, R3, l3), F32),
-        pairs=pltpu.VMEM((max(L0, l2) // 128, 160, 128), F32),
+        pairs=pltpu.VMEM((max(L0, l2) // 128, 168, 128), F32),
         agg=pltpu.VMEM((nx // 2, 2 * ny * nz), jnp.int32),
         prol1=pltpu.VMEM((l2, L1), BF16),
         zero16=pltpu.VMEM((2, 4, 16, 128), F32),

time: 62.8 us -> 62.8 us (level)
  no operation moved by 1% of the time
where the time goes in v5:
time: 62.8 us; the launch traced here: 62.6 us
  Pallas kernels  62 us (99%)
  local copies, waits for them, and re-layouts  0.63 us (1%)
    pallas_call x1, Pallas kernels, body(): pl.pallas_call(kernel, out_shape=pltpu.VMEM((8, 16, 128), F32), in_specs=...  62 us

profile of v5, /device:TPU:1, one launch (start us, length us, event | category | flops | bytes accessed | tf_op | source)
XLA Modules:
  0.0 62.6 jit_solution(17578528040311650913)
XLA Ops:
  0.0 62.0 %shard_map.172 = f32[8,16,128]{2,1,0:T(8,128)S(1)} custom-call(f32[8,16,128]{2,1,0:T(8,128)} %rhs_hbm.1, f32[8,16,128]{2,1,0:T(8,128)} %coef_hbm.1, s32[4,128]{1,0:T(4,128)} %bitcast.1, bf16[384,128]{1,0:T(8,128)(2,1)} %constant.30.clone.rest_0_, bf16[384,384]{1,0:T(8,128)(2,1)} %constant.31.clone.rest_1_, bf16[32,384]{1,0:T(8,128)(2,1)} %constant.32.clone.rest_2_, ...), custom_call_target="tpu_custom_call" | custom-call | tf_op jit(solution)/shard_map/pallas_call | solution.py:753
  62.0 0.6 %copy.20 = f32[8,16,128]{2,1,0:T(8,128)} copy(f32[8,16,128]{2,1,0:T(8,128)S(1)} %shard_map.172) | data formatting | bytes 131072
